TPU v7x, 32 devices: a whole 2x2x4 slice. The times are simulated.
32 devices in a mesh: dp: 8 (over z, x), mp: 4 (over y, core).
Axes of the slice: x: 2, y: 2, z: 4, core: 2. Of those that a mesh axis runs over, the one named last changes fastest.
Arguments:
- conv_in: bfloat16 [16384, 1024], P('dp'), may hold values from -6 to 6
- conv_weight: bfloat16 [1024, 512], P(None, 'mp'), may hold values from -0.1875 to 0.1875
- feature_gain: float32 [512], replicated, may hold values from 0.1 to 1.9
- proj_weight: bfloat16 [512, 1024], replicated, may hold values from -0.25 to 0.25
- block_gain: float32 [1024], replicated, may hold values from 0.1 to 1.9
- w_in: bfloat16 [1024, 4096], P(None, 'mp'), may hold values from -0.1875 to 0.1875
- w_out: bfloat16 [1024, 4096], P(None, 'mp'), may hold values from -0.09375 to 0.09375
- cotangent: bfloat16 [16384, 1024], P('dp'), may hold values from -0.0625 to 0.0625
- send_index: int32 [16384], P('dp'), may hold values from 0 to 2047, as said below
- slot_valid: int32 [16384], P('dp'), may hold values from 0 to 1, as said below
Outputs:
- grad_conv_weight: float32 [1024, 512], P('dp', 'mp')
- grad_proj_weight: float32 [512, 1024], P('dp', 'mp')
- grad_w_in: float32 [1024, 4096], P('dp', 'mp')
- grad_w_out: float32 [1024, 4096], P('dp', 'mp')
Inputs may be any that keep to these rules, and one draw needn't show every extreme that they name: `send_index`: the 2048 entries held by one index of dp are a permutation of 0 to 2047; entry e * 256 + j names the local frame sent to slot j of index e. `slot_valid`: slot j of the block from source s on index e is 1 exactly when the frame it receives lies inside the source's clips; a source's frames inside clips are its first ones, at least 512 of them, and some source has all 2048.
All inputs are finite; a program needn't handle non-finite values.
Results may differ from a plain program's by a relative error of at most 0.015.
Values may be sent and summed in bfloat16 or wider, within the bound.
A program may use at most 128 MiB of HBM per device.

v0:
```python
import jax
import jax.numpy as jnp
from jax import lax
from jax.sharding import PartitionSpec as P

EPSILON = 1e-05
SQRT_HALF = 0.7071067811865476
INV_SQRT_TWO_PI = 0.3989422804014327


def gelu_exact(values):
    return 0.5 * values * (1.0 + lax.erf(values * SQRT_HALF))


def gelu_slope(values):
    return 0.5 * (1.0 + lax.erf(values * SQRT_HALF)) + values * INV_SQRT_TWO_PI * jnp.exp(
        -0.5 * values * values
    )


def normalize(values):
    row_mean = jnp.mean(values, axis=-1, keepdims=True)
    centred = values - row_mean
    inv_std = lax.rsqrt(jnp.mean(centred * centred, axis=-1, keepdims=True) + EPSILON)
    return (centred * inv_std, inv_std)


def norm_back(upstream, normed, inv_std, gain_row):
    scaled = upstream * gain_row
    first_mean = jnp.mean(scaled, axis=-1, keepdims=True)
    second_mean = jnp.mean(scaled * normed, axis=-1, keepdims=True)
    return inv_std * (scaled - first_mean - normed * second_mean)


def contract_rows(left, right):
    return lax.dot_general(
        left, right, (((0,), (0,)), ((), ())), preferred_element_type=jnp.float32
    )


def contract_cols(left, right):
    return lax.dot_general(
        left, right, (((1,), (1,)), ((), ())), preferred_element_type=jnp.float32
    )


def on_device(
    conv_in,
    conv_weight,
    feature_gain,
    proj_weight,
    block_gain,
    w_in,
    w_out,
    cotangent,
    send_index,
    slot_valid,
):
    frames = conv_in.shape[0]
    shards = lax.axis_size("mp")
    member = lax.axis_index("mp")
    chan_part = conv_weight.shape[1]
    width_part = proj_weight.shape[1] // shards
    pre_act = jnp.dot(conv_in, conv_weight, preferred_element_type=jnp.float32)
    features = gelu_exact(pre_act).astype(jnp.bfloat16)
    outgoing = jnp.take(features, send_index, axis=0)
    arrived = lax.all_to_all(outgoing, "dp", split_axis=0, concat_axis=0, tiled=True)
    packed = lax.all_gather(arrived, "mp", axis=1, tiled=True)
    feat_norm, feat_inv = normalize(packed.astype(jnp.float32))
    feat_ln = (feat_norm * feature_gain).astype(jnp.bfloat16)
    hidden = jnp.dot(feat_ln, proj_weight, preferred_element_type=jnp.float32)
    hid_norm, hid_inv = normalize(hidden)
    hid_ln = (hid_norm * block_gain).astype(jnp.bfloat16)
    upward = jnp.dot(hid_ln, w_in, preferred_element_type=jnp.float32)
    active = gelu_exact(upward).astype(jnp.bfloat16)
    masked_cot = cotangent * slot_valid.astype(jnp.bfloat16)[:, None]
    grad_active = jnp.dot(masked_cot, w_out, preferred_element_type=jnp.float32)
    grad_upward = (grad_active * gelu_slope(upward)).astype(jnp.bfloat16)
    out_term = contract_rows(masked_cot, active)
    in_term = contract_rows(hid_ln, grad_upward)
    partial_value = contract_cols(grad_upward, w_in)
    share_rows = frames // shards
    first_row = member * share_rows
    share_normed = lax.psum_scatter(
        partial_value.astype(jnp.bfloat16), "mp", scatter_dimension=0, tiled=True
    ).astype(jnp.float32)
    share_cot = lax.dynamic_slice_in_dim(masked_cot, first_row, share_rows, 0).astype(jnp.float32)
    share_norm = lax.dynamic_slice_in_dim(hid_norm, first_row, share_rows, 0)
    share_inv = lax.dynamic_slice_in_dim(hid_inv, first_row, share_rows, 0)
    share_grad = (share_cot + norm_back(share_normed, share_norm, share_inv, block_gain)).astype(
        jnp.bfloat16
    )
    grad_hidden = lax.all_gather(share_grad, "mp", axis=0, tiled=True)
    grad_cols = lax.dynamic_slice_in_dim(grad_hidden, member * width_part, width_part, 1)
    proj_term = contract_rows(feat_ln, grad_cols)
    grad_feat_ln = contract_cols(grad_hidden, proj_weight)
    grad_packed = norm_back(grad_feat_ln, feat_norm, feat_inv, feature_gain)
    grad_mine = lax.dynamic_slice_in_dim(grad_packed, member * chan_part, chan_part, 1).astype(
        jnp.bfloat16
    )
    returned = lax.all_to_all(grad_mine, "dp", split_axis=0, concat_axis=0, tiled=True)
    grad_features = (
        jnp.zeros((frames, chan_part), jnp.float32).at[send_index].add(returned.astype(jnp.float32))
    )
    grad_pre = (grad_features * gelu_slope(pre_act)).astype(jnp.bfloat16)
    conv_term = contract_rows(conv_in, grad_pre)
    grads = (
        lax.psum_scatter(
            conv_term.astype(jnp.bfloat16), "dp", scatter_dimension=0, tiled=True
        ).astype(jnp.float32),
        lax.psum_scatter(
            proj_term.astype(jnp.bfloat16), "dp", scatter_dimension=0, tiled=True
        ).astype(jnp.float32),
        lax.psum_scatter(
            in_term.astype(jnp.bfloat16), "dp", scatter_dimension=0, tiled=True
        ).astype(jnp.float32),
        lax.psum_scatter(
            out_term.astype(jnp.bfloat16), "dp", scatter_dimension=0, tiled=True
        ).astype(jnp.float32),
    )
    result = (grads[0], grads[1], grads[2], grads[3])
    return result


def solution(mesh):
    placed = (
        P("dp", None),
        P(None, "mp"),
        P(),
        P(),
        P(),
        P(None, "mp"),
        P(None, "mp"),
        P("dp", None),
        P("dp"),
        P("dp"),
    )
    return jax.shard_map(
        on_device,
        mesh=mesh,
        in_specs=placed,
        out_specs=(P("dp", "mp"), P("dp", "mp"), P("dp", "mp"), P("dp", "mp")),
        check_vma=False,
    )
```

profile of v0, /device:TPU:0, one launch (start us, length us, event | category | flops | bytes accessed | tf_op | source)
XLA Modules:
  0.0 467.2 jit_solution(15901624684417455059)
XLA Ops:
  8.8 4.4 multiply_convert_fusion.6
  13.2 6.2 %gather_fusion = bf16[2048,128]{1,0:T(8,128)(2,1)S(1)} fusion(bf16[2048,128]{1,0:T(8,128)(2,1)S(1)} %get-tuple-element.19, s32[2048]{0:T(1024)S(1)} %get-tuple-element.17), kind=kCustom, calls=%fused_computation | custom fusion | bytes 1056768 | tf_op jit(solution)/shard_map/jit(_take)/gather | solution.py:66
  19.8 21.7 %all_to_all.18 = bf16[8,256,128]{2,1,0:T(8,128)(2,1)} all-to-all(bf16[8,256,128]{2,1,0:T(8,128)(2,1)S(1)} %broadcast_select_fusion), channel_id=1, replica_groups=mesh['dp'=8,'mp'=4] {'dp'}, dimensions={0} | all-to-all | bytes 1048576 | tf_op jit(solution)/shard_map/all_to_all | solution.py:67
  41.6 6.5 %copy.17 = bf16[2048,1024]{0,1:T(8,128)(2,1)} copy(bf16[2048,1024]{1,0:T(8,128)(2,1)} %param.17) | data formatting | bytes 8388608 | tf_op args[7]
  48.1 4.6 broadcast_multiply_fusion
  52.6 10.9 %all-gather.3.cloned.1.call-done = bf16[2048,512]{1,0:T(8,128)(2,1)} async-done(((bf16[2048,128]{1,0:T(8,128)(2,1)}), bf16[2048,512]{1,0:T(8,128)(2,1)}) %all-gather.3.cloned.1.call-update) | async-done | bytes 2097168 | tf_op jit(solution)/shard_map/all_gather | solution.py:68
  63.5 2.1 convert_reduce_fusion
  65.6 2.5 fusion.7
  68.1 2.9 fusion.39
  71.9 1.9 subtract_multiply_fusion
  73.8 4.9 %fusion.35 = f32[2048,1024]{1,0:T(8,128)S(1)} fusion(bf16[1024,1024]{1,0:T(8,128)(2,1)S(1)} %copy-done, f32[2048,1024]{0,1:T(8,128)S(1)} %subtract_multiply_fusion, f32[1024]{0:T(1024)S(1)} %copy-done.7), kind=kOutput, calls=%fused_computation.72 | convolution fusion | flops 4299161600 | bytes 18878464 | tf_op jit(solution)/shard_map/dot_general | solution.py:74
  79.7 7.3 %fusion.4 = bf16[2048,1024]{1,0:T(8,128)(2,1)S(1)} fusion(f32[2048,1024]{1,0:T(8,128)S(1)} %fusion.35, bf16[2048,1024]{0,1:T(8,128)(2,1)S(1)} %copy-done.5, bf16[1024,1024]{1,0:T(8,128)(2,1)S(1)} %copy-done.9), kind=kOutput, calls=%fused_computation.7 | convolution fusion | flops 4315938816 | bytes 18874368 | tf_op jit(solution)/shard_map/dot_general | solution.py:77
  87.1 1.9 copy-done.13
  89.0 6.1 %convolution_convert_fusion = bf16[2048,1024]{0,1:T(8,128)(2,1)} fusion(bf16[2048,1024]{1,0:T(8,128)(2,1)S(1)} %fusion.4, bf16[1024,1024]{1,0:T(8,128)(2,1)S(1)} %copy-done), kind=kOutput, calls=%fused_computation.22 | convolution fusion | flops 4297064448 | bytes 10485760 | tf_op jit(solution)/shard_map/dot_general | solution.py:42
  95.2 44.4 %reduce-scatter.8.cloned.1.call-done = bf16[512,1024]{0,1:T(8,128)(2,1)} async-done(((bf16[2048,1024]{0,1:T(8,128)(2,1)}), bf16[512,1024]{0,1:T(8,128)(2,1)}) %reduce-scatter.8.cloned.1.call-update) | async-done | bytes 1048592 | tf_op jit(solution)/shard_map/reduce_scatter | solution.py:84
  139.7 2.3 fusion.10
  142.0 3.8 add_convert_fusion
  145.9 9.3 %fusion.11 = bf16[1024,1024]{1,0:T(8,128)(2,1)} fusion(bf16[2048,1024]{0,1:T(8,128)(2,1)} %broadcast_multiply_fusion, f32[2048,1024]{1,0:T(8,128)} %copy-done.12), kind=kOutput, calls=%fused_computation.30 | convolution fusion | flops 4306501632 | bytes 14680064 | tf_op jit(solution)/shard_map/dot_general | solution.py:36
  155.3 10.7 %convolution_convert_fusion.1 = bf16[1024,1024]{1,0:T(8,128)(2,1)} fusion(bf16[2048,1024]{1,0:T(8,128)(2,1)} %copy-done.13, f32[2048,1024]{0,1:T(8,128)} %copy-done.2, f32[1024]{0:T(1024)S(1)} %copy-done.7), kind=kOutput, calls=%fused_computation.29 | convolution fusion | flops 4300210176 | bytes 14684160 | tf_op jit(solution)/shard_map/dot_general | solution.py:36
  166.0 14.5 %all-gather.5.cloned.1.call-done = bf16[2048,1024]{0,1:T(8,128)(2,1)} async-done(((bf16[512,1024]{0,1:T(8,128)(2,1)}), bf16[2048,1024]{0,1:T(8,128)(2,1)}) %all-gather.5.cloned.1.call-update) | async-done | bytes 4194320 | tf_op jit(solution)/shard_map/all_gather | solution.py:93
  180.5 5.6 %fusion.38 = (f32[2048]{0:T(1024)S(1)}, f32[2048]{0:T(1024)S(1)}, f32[2048,512]{1,0:T(8,128)S(1)}, f32[2048,512]{1,0:T(8,128)S(1)}) fusion(f32[2048]{0:T(1024)S(1)} %add_rsqrt_fusion.1, f32[2048]{0:T(1024)S(1)} %broadcast_multiply_fusion.4, bf16[2048,512]{1,0:T(8,128)(2,1)S(1)} %copy-done.4, f32[512]{0:T(512)S(1)} %copy-done.11, ...), kind=kOutput, calls=%fused_computation.73 | convolution fusion | flops 2154819584 | bytes 15763456 | tf_op jit(solution)/shard_map/dot_general | solution.py:42
  187.9 5.5 %all-to-all-start.1 = ((bf16[8,256,128]{2,1,0:T(8,128)(2,1)}), bf16[8,256,128]{2,1,0:T(8,128)(2,1)}, u32[]{:S(2)}, u32[]{:S(2)}) async-start(bf16[8,256,128]{2,1,0:T(8,128)(2,1)} %bitcast.2), calls=%async_computation.2 | async-start | bytes 1048576 | tf_op jit(solution)/shard_map/all_to_all | solution.py:101
  193.4 3.5 convolution_convert_fusion.2
  197.0 23.2 %all-to-all-done.1 = bf16[8,256,128]{2,1,0:T(8,128)(2,1)} async-done(((bf16[8,256,128]{2,1,0:T(8,128)(2,1)}), bf16[8,256,128]{2,1,0:T(8,128)(2,1)}, u32[]{:S(2)}, u32[]{:S(2)}) %all-to-all-start.1) | async-done | bytes 524320 | tf_op jit(solution)/shard_map/all_to_all | solution.py:101
  220.2 12.8 %scatter_custom_fusion = f32[2048,128]{1,0:T(8,128)} fusion(s32[2048]{0:T(1024)S(1)} %get-tuple-element.18, bf16[2048,128]{1,0:T(8,128)(2,1)} %bitcast.6, f32[]{:T(128)} %constant.18.clone.1), kind=kCustom, calls=%fused_computation.45 | custom fusion | flops 524288 | bytes 1572868 | tf_op jit(solution)/shard_map/scatter-add | solution.py:103
  233.0 3.8 fusion.12
  237.8 21.5 %reduce-scatter.14.cloned.1.call-done = bf16[128,1024]{1,0:T(8,128)(2,1)} async-done(((bf16[1024,1024]{1,0:T(8,128)(2,1)}), bf16[128,1024]{1,0:T(8,128)(2,1)}) %reduce-scatter.14.cloned.1.call-update) | async-done | bytes 262160 | tf_op jit(solution)/shard_map/reduce_scatter | solution.py:117
  259.3 1.8 convert_element_type.95
  261.1 69.0 %reduce-scatter.12.cloned.1.call-done = bf16[128,1024]{1,0:T(8,128)(2,1)} async-done(((bf16[1024,1024]{1,0:T(8,128)(2,1)}), bf16[128,1024]{1,0:T(8,128)(2,1)}) %reduce-scatter.12.cloned.1.call-update) | async-done | bytes 262160 | tf_op jit(solution)/shard_map/reduce_scatter | solution.py:114
  330.1 1.8 convert_element_type.92
  331.9 62.5 %reduce-scatter.10.cloned.1.call-done = bf16[64,256]{1,0:T(8,128)(2,1)} async-done(((bf16[512,256]{1,0:T(8,128)(2,1)}), bf16[64,256]{1,0:T(8,128)(2,1)}) %reduce-scatter.10.cloned.1.call-update) | async-done | bytes 32784 | tf_op jit(solution)/shard_map/reduce_scatter | solution.py:111
  395.7 63.1 %reduce-scatter.16.cloned.1.call-done = bf16[128,128]{1,0:T(8,128)(2,1)} async-done(((bf16[1024,128]{1,0:T(8,128)(2,1)}), bf16[128,128]{1,0:T(8,128)(2,1)}) %reduce-scatter.16.cloned.1.call-update) | async-done | bytes 32784
  (60 shorter events, 9.8 us)
Async XLA Ops:
  7.2 66.6 %copy-start = (bf16[1024,1024]{1,0:T(8,128)(2,1)S(1)}, bf16[1024,1024]{1,0:T(8,128)(2,1)}, u32[]{:S(2)}) copy-start(bf16[1024,1024]{1,0:T(8,128)(2,1)} %param.15) | copy-start | bytes 6291460
  7.2 56.3 %all-gather.3.cloned.1.call-start = ((), (), s32[]{:S(2)}) async-start(), calls=%async_computation.7 | async-start | bytes 2621440 | tf_op jit(solution)/shard_map/all_gather | solution.py:68
  13.2 28.3 %copy-start.8 = (s32[2048]{0:T(1024)S(1)}, s32[2048]{0:T(1024)}, u32[]{:S(2)}) copy-start(s32[2048]{0:T(1024)} %param.19) | copy-start | bytes 24580
  41.5 98.2 %reduce-scatter.8.cloned.1.call-start = ((), (), s32[]{:S(2)}) async-start(), calls=%async_computation.8 | async-start | bytes 5242880 | tf_op jit(solution)/shard_map/reduce_scatter | solution.py:84
  52.6 15.5 %copy-start.10 = (bf16[512,1024]{1,0:T(8,128)(2,1)S(1)}, bf16[512,1024]{1,0:T(8,128)(2,1)}, u32[]{:S(2)}) copy-start(bf16[512,1024]{1,0:T(8,128)(2,1)} %param.13) | copy-start | bytes 3145732
  52.6 15.5 %copy-start.11 = (f32[512]{0:T(512)S(1)}, f32[512]{0:T(512)}, u32[]{:S(2)}) copy-start(f32[512]{0:T(512)} %param.12) | copy-start | bytes 6148
  63.5 4.6 copy-start.3
  71.9 1.9 copy-start.7
  73.8 4.9 %copy-start.2 = (f32[2048,1024]{0,1:T(8,128)}, f32[2048,1024]{0,1:T(8,128)S(1)}, u32[]{:S(2)}) copy-start(f32[2048,1024]{0,1:T(8,128)S(1)} %subtract_multiply_fusion) | copy-start | bytes 25165828
  73.8 5.2 %copy-start.5 = (bf16[2048,1024]{0,1:T(8,128)(2,1)S(1)}, bf16[2048,1024]{0,1:T(8,128)(2,1)}, u32[]{:S(2)}) copy-start(bf16[2048,1024]{0,1:T(8,128)(2,1)} %broadcast_multiply_fusion) | copy-start | bytes 12582916
  73.8 5.9 %copy-start.9 = (bf16[1024,1024]{1,0:T(8,128)(2,1)S(1)}, bf16[1024,1024]{1,0:T(8,128)(2,1)}, u32[]{:S(2)}) copy-start(bf16[1024,1024]{1,0:T(8,128)(2,1)} %param.16) | copy-start | bytes 6291460
  79.7 7.3 %copy-start.12 = (f32[2048,1024]{1,0:T(8,128)}, f32[2048,1024]{1,0:T(8,128)S(1)}, u32[]{:S(2)}) copy-start(f32[2048,1024]{1,0:T(8,128)S(1)} %fusion.35) | copy-start | bytes 25165828
  87.1 2.0 copy-start.13
  95.1 85.4 %all-gather.5.cloned.1.call-start = ((), (), s32[]{:S(2)}) async-start(), calls=%async_computation.9 | async-start | bytes 5242880 | tf_op jit(solution)/shard_map/all_gather | solution.py:93
  145.9 113.4 %reduce-scatter.14.cloned.1.call-start = ((), (), s32[]{:S(2)}) async-start(), calls=%async_computation.12 | async-start | bytes 2359296 | tf_op jit(solution)/shard_map/reduce_scatter | solution.py:117
  155.2 25.3 %copy-start.4 = (bf16[2048,512]{1,0:T(8,128)(2,1)S(1)}, bf16[2048,512]{1,0:T(8,128)(2,1)}, u32[]{:S(2)}) copy-start(bf16[2048,512]{1,0:T(8,128)(2,1)} %all-gather.3.cloned.1.call-done) | copy-start | bytes 6291460
  155.2 174.8 %reduce-scatter.12.cloned.1.call-start = ((), (), s32[]{:S(2)}) async-start(), calls=%async_computation.11 | async-start | bytes 2359296 | tf_op jit(solution)/shard_map/reduce_scatter | solution.py:114
  187.9 32.3 %all-to-all-start.1 = ((bf16[8,256,128]{2,1,0:T(8,128)(2,1)}), bf16[8,256,128]{2,1,0:T(8,128)(2,1)}, u32[]{:S(2)}, u32[]{:S(2)}) async-start(bf16[8,256,128]{2,1,0:T(8,128)(2,1)} %bitcast.2), calls=%async_computation.2 | async-start | bytes 1048576 | tf_op jit(solution)/shard_map/all_to_all | solution.py:101
  193.4 200.9 %reduce-scatter.10.cloned.1.call-start = ((), (), s32[]{:S(2)}) async-start(), calls=%async_computation.10 | async-start | bytes 294912 | tf_op jit(solution)/shard_map/reduce_scatter | solution.py:111
  193.4 39.6 %copy-start.6 = (f32[2048,128]{1,0:T(8,128)S(1)}, f32[2048,128]{1,0:T(8,128)}, u32[]{:S(2)}) copy-start(f32[2048,128]{1,0:T(8,128)} %get-tuple-element.20) | copy-start | bytes 3145732
  196.9 261.8 %reduce-scatter.16.cloned.1.call-start = ((), (), s32[]{:S(2)}) async-start(), calls=%async_computation.13 | async-start | bytes 294912
  233.0 227.3 %copy-start.1 = (bf16[1024,1024]{1,0:T(8,128)(2,1)S(1)}, bf16[1024,1024]{1,0:T(8,128)(2,1)}, u32[]{:S(2)}) copy-start(bf16[1024,1024]{1,0:T(8,128)(2,1)} %param.15) | copy-start | bytes 6291460
Sparse Core Ops, SparseCore 0:
  41.6 21.8 all-gather.2
  95.2 44.3 reduce-scatter.7
  146.0 34.4 all-gather.4
  183.9 75.3 reduce-scatter.13
  262.7 67.3 reduce-scatter.11
  333.2 61.0 reduce-scatter.9
  397.6 61.0 reduce-scatter.15
where the time goes:
time: 468 us; the launch traced here: 467 us
  waiting for transfers between devices  309 us (66%)
  matrix products  58.5 us (12%)
  other arithmetic  39.5 us (8%)
  blocking collectives  21.7 us (5%)
  local copies, waits for them, and re-layouts  18.2 us (4%)
  between operations  14.4 us (3%)
  starting transfers between devices  5.8 us (1%)
    reduce_scatter x1, waiting for transfers between devices, on_device(): lax.psum_scatter(in_term.astype(jnp.bfloat16), 'dp', scatter_dimension=0,...  69 us
    unnamed x8, waiting for transfers between devices  63.2 us
    reduce_scatter x1, waiting for transfers between devices, on_device(): lax.psum_scatter(proj_term.astype(jnp.bfloat16), 'dp', scatter_dimension=...  62.5 us
    reduce_scatter x1, waiting for transfers between devices, on_device(): lax.psum_scatter(partial_value.astype(jnp.bfloat16), 'mp', scatter_dimens...  44.4 us
    dot_general x4, matrix products, contract_rows(): lax.dot_general(left, right, (((0,), (0,)), ((), ())), preferred_element_...  27.3 us
    all_to_all x1, waiting for transfers between devices, on_device(): lax.all_to_all(grad_mine, 'dp', split_axis=0, concat_axis=0, tiled=True)  23.2 us
    all_to_all x1, blocking collectives, on_device(): lax.all_to_all(outgoing, 'dp', split_axis=0, concat_axis=0, tiled=True)  21.7 us
    reduce_scatter x1, waiting for transfers between devices, on_device(): lax.psum_scatter(out_term.astype(jnp.bfloat16), 'dp', scatter_dimension=0...  21.5 us
  transfers between devices with their start and end apart: 8, of which 8 were waited for; matrix products, arithmetic and copies ran while one was open for 14% of the time, Pallas kernels for 0%

commit v1 on v0

--- a/solution.py
+++ b/solution.py
@@ -1,11 +1,16 @@
+import functools
+
 import jax
 import jax.numpy as jnp
 from jax import lax
+from jax.experimental import pallas as pl
+from jax.experimental.pallas import tpu as pltpu
 from jax.sharding import PartitionSpec as P
 
 EPSILON = 1e-05
 SQRT_HALF = 0.7071067811865476
 INV_SQRT_TWO_PI = 0.3989422804014327
+VMEM_LIMIT = 48 * 1024 * 1024
 
 
 def gelu_exact(values):
@@ -42,6 +47,114 @@
     return lax.dot_general(
         left, right, (((1,), (1,)), ((), ())), preferred_element_type=jnp.float32
     )
+
+
+def scatter_sum_kernel(parts, count, *refs):
+    ins, outs = refs[:count], refs[count : 2 * count]
+    first_in, staged, second_in = (refs[(2 + i) * count : (3 + i) * count] for i in range(3))
+    send_one, recv_one, send_two, recv_two = refs[5 * count :]
+    half = parts // 2
+    me = lax.axis_index("dp")
+    parity = lax.rem(me, 2)
+    place = me // 2
+    partner = me + 1 - 2 * parity
+    order = list(range(1, half)) + [0]
+
+    barrier = pltpu.get_barrier_semaphore()
+    pl.semaphore_signal(
+        barrier, inc=1, device_id={"dp": partner}, device_id_type=pl.DeviceIdType.MESH
+    )
+    for k in range(1, half):
+        peer = 2 * lax.rem(place + k, half) + parity
+        pl.semaphore_signal(
+            barrier, inc=1, device_id={"dp": peer}, device_id_type=pl.DeviceIdType.MESH
+        )
+    pl.semaphore_wait(barrier, half)
+
+    def each_tile(rows, body):
+        def step(i, carry):
+            body(pl.ds(pl.multiple_of(i * 16, 16), 16), i)
+            return carry
+
+        lax.fori_loop(0, rows // 16, step, 0)
+
+    ones, twos = {}, {}
+    for k in order:
+        target = lax.rem(place + k, half)
+        for i in range(count):
+            rows = outs[i].shape[0]
+            start = pl.multiple_of((2 * target + 1 - parity) * rows, rows)
+            ones[k, i] = pltpu.make_async_remote_copy(
+                src_ref=ins[i].at[pl.ds(start, rows)],
+                dst_ref=first_in[i].at[k],
+                send_sem=send_one.at[i, k],
+                recv_sem=recv_one.at[i, k],
+                device_id={"dp": partner},
+                device_id_type=pl.DeviceIdType.MESH,
+            )
+            ones[k, i].start()
+    for k in order:
+        target = lax.rem(place + k, half)
+        for i in range(count):
+            rows = outs[i].shape[0]
+            base = (2 * target + parity) * rows
+            ones[k, i].wait_recv()
+
+            def add(tile, step, i=i, k=k, base=base):
+                mine = ins[i][pl.ds(pl.multiple_of(base + step * 16, 16), 16), :]
+                total = mine.astype(jnp.float32) + first_in[i][k, tile, :].astype(jnp.float32)
+                if k:
+                    staged[i][k, tile, :] = total.astype(jnp.bfloat16)
+                else:
+                    outs[i][tile, :] = total
+
+            each_tile(rows, add)
+            if k:
+                twos[k, i] = pltpu.make_async_remote_copy(
+                    src_ref=staged[i].at[k],
+                    dst_ref=second_in[i].at[k],
+                    send_sem=send_two.at[i, k],
+                    recv_sem=recv_two.at[i, k],
+                    device_id={"dp": 2 * target + parity},
+                    device_id_type=pl.DeviceIdType.MESH,
+                )
+                twos[k, i].start()
+    for i in range(count):
+        for k in range(1, half):
+            twos[k, i].wait_recv()
+
+        def gather(tile, step, i=i):
+            total = outs[i][tile, :]
+            for k in range(1, half):
+                total = total + second_in[i][k, tile, :].astype(jnp.float32)
+            outs[i][tile, :] = total
+
+        each_tile(outs[i].shape[0], gather)
+    for copy in list(ones.values()) + list(twos.values()):
+        copy.wait_send()
+
+
+def scatter_sum(terms, collective_id):
+    parts = lax.axis_size("dp")
+    half = parts // 2
+    count = len(terms)
+    blocks = [(term.shape[0] // parts, term.shape[1]) for term in terms]
+    slots = [pltpu.VMEM((half,) + block, jnp.bfloat16) for block in blocks]
+    sent = sum(term.size * 2 for term in terms)
+    return pl.pallas_call(
+        functools.partial(scatter_sum_kernel, parts, count),
+        out_shape=[jax.ShapeDtypeStruct(block, jnp.float32) for block in blocks],
+        in_specs=[pl.BlockSpec(memory_space=pltpu.VMEM)] * count,
+        out_specs=[pl.BlockSpec(memory_space=pltpu.VMEM)] * count,
+        scratch_shapes=slots * 3 + [pltpu.SemaphoreType.DMA((count, half))] * 4,
+        compiler_params=pltpu.CompilerParams(
+            collective_id=collective_id, has_side_effects=True, vmem_limit_bytes=VMEM_LIMIT
+        ),
+        cost_estimate=pl.CostEstimate(
+            flops=sent * 4000, bytes_accessed=sent * 40, transcendentals=0
+        ),
+        name="scatter_sum",
+    )(*terms)
 
 
 def on_device(
@@ -59,11 +172,10 @@
     frames = conv_in.shape[0]
     shards = lax.axis_size("mp")
     member = lax.axis_index("mp")
-    chan_part = conv_weight.shape[1]
-    width_part = proj_weight.shape[1] // shards
     pre_act = jnp.dot(conv_in, conv_weight, preferred_element_type=jnp.float32)
     features = gelu_exact(pre_act).astype(jnp.bfloat16)
-    outgoing = jnp.take(features, send_index, axis=0)
+    choose = (send_index[:, None] == jnp.arange(frames, dtype=send_index.dtype)).astype(jnp.bfloat16)
+    outgoing = jnp.dot(choose, features, preferred_element_type=jnp.float32).astype(jnp.bfloat16)
     arrived = lax.all_to_all(outgoing, "dp", split_axis=0, concat_axis=0, tiled=True)
     packed = lax.all_gather(arrived, "mp", axis=1, tiled=True)
     feat_norm, feat_inv = normalize(packed.astype(jnp.float32))
@@ -84,40 +196,34 @@
     share_normed = lax.psum_scatter(
         partial_value.astype(jnp.bfloat16), "mp", scatter_dimension=0, tiled=True
     ).astype(jnp.float32)
+    in_grad, out_grad = scatter_sum(
+        [in_term.astype(jnp.bfloat16), out_term.astype(jnp.bfloat16)], 1
+    )
+    share_normed, in_grad, out_grad = lax.optimization_barrier((share_normed, in_grad, out_grad))
     share_cot = lax.dynamic_slice_in_dim(masked_cot, first_row, share_rows, 0).astype(jnp.float32)
     share_norm = lax.dynamic_slice_in_dim(hid_norm, first_row, share_rows, 0)
     share_inv = lax.dynamic_slice_in_dim(hid_inv, first_row, share_rows, 0)
     share_grad = (share_cot + norm_back(share_normed, share_norm, share_inv, block_gain)).astype(
         jnp.bfloat16
     )
-    grad_hidden = lax.all_gather(share_grad, "mp", axis=0, tiled=True)
-    grad_cols = lax.dynamic_slice_in_dim(grad_hidden, member * width_part, width_part, 1)
-    proj_term = contract_rows(feat_ln, grad_cols)
-    grad_feat_ln = contract_cols(grad_hidden, proj_weight)
-    grad_packed = norm_back(grad_feat_ln, feat_norm, feat_inv, feature_gain)
-    grad_mine = lax.dynamic_slice_in_dim(grad_packed, member * chan_part, chan_part, 1).astype(
+    share_feat = lax.dynamic_slice_in_dim(feat_ln, first_row, share_rows, 0)
+    share_feat_norm = lax.dynamic_slice_in_dim(feat_norm, first_row, share_rows, 0)
+    share_feat_inv = lax.dynamic_slice_in_dim(feat_inv, first_row, share_rows, 0)
+    grad_feat_ln = contract_cols(share_grad, proj_weight)
+    grad_packed = norm_back(grad_feat_ln, share_feat_norm, share_feat_inv, feature_gain).astype(
         jnp.bfloat16
     )
+    proj_term = contract_rows(share_feat, share_grad)
+    proj_part = lax.psum_scatter(
+        proj_term.astype(jnp.bfloat16), "mp", scatter_dimension=1, tiled=True
+    )
+    grad_mine = lax.all_to_all(grad_packed, "mp", split_axis=1, concat_axis=0, tiled=True)
     returned = lax.all_to_all(grad_mine, "dp", split_axis=0, concat_axis=0, tiled=True)
-    grad_features = (
-        jnp.zeros((frames, chan_part), jnp.float32).at[send_index].add(returned.astype(jnp.float32))
-    )
+    grad_features = contract_rows(choose, returned)
     grad_pre = (grad_features * gelu_slope(pre_act)).astype(jnp.bfloat16)
     conv_term = contract_rows(conv_in, grad_pre)
-    grads = (
-        lax.psum_scatter(
-            conv_term.astype(jnp.bfloat16), "dp", scatter_dimension=0, tiled=True
-        ).astype(jnp.float32),
-        lax.psum_scatter(
-            proj_term.astype(jnp.bfloat16), "dp", scatter_dimension=0, tiled=True
-        ).astype(jnp.float32),
-        lax.psum_scatter(
-            in_term.astype(jnp.bfloat16), "dp", scatter_dimension=0, tiled=True
-        ).astype(jnp.float32),
-        lax.psum_scatter(
-            out_term.astype(jnp.bfloat16), "dp", scatter_dimension=0, tiled=True
-        ).astype(jnp.float32),
-    )
+    conv_grad, proj_grad = scatter_sum([conv_term.astype(jnp.bfloat16), proj_part], 2)
+    grads = (conv_grad, proj_grad, in_grad, out_grad)
     result = (grads[0], grads[1], grads[2], grads[3])
     return result
 

time: 468 us -> 238 us (0.51)
  waiting for transfers between devices: 309 us -> 24.7 us
  Pallas kernels: 0 us -> 68.8 us
  other arithmetic: 39.5 us -> 21.6 us
  blocking collectives: 21.7 us -> 33.5 us
    reduce_scatter x3 -> x1, waiting for transfers between devices: 153 us -> 0.02 us  [on_device(): lax.psum_scatter(proj_term.astype(jnp.bfloat16), 'mp', scatter_dimension=...]
    pallas_call x0 -> x2, Pallas kernels: none -> 68.8 us  [scatter_sum(): pl.pallas_call(functools.partial(scatter_sum_kernel, parts, count), out_s...]
    unnamed x8 -> x3, waiting for transfers between devices: 63.2 us -> 0.05 us
    reduce_scatter x1, waiting for transfers between devices: 44.4 us -> 0.02 us  [on_device(): lax.psum_scatter(partial_value.astype(jnp.bfloat16), 'mp', scatter_dimens...]
    all_gather x1 -> x0, waiting for transfers between devices: 14.5 us -> none  [on_device(): grad_hidden = lax.all_gather(share_grad, 'mp', axis=0, tiled=True)]
    scatter-add x1 -> x0, other arithmetic: 12.8 us -> none  [on_device(): jnp.zeros((frames, chan_part), jnp.float32).at[send_index]]
    all_to_all x0 -> x1, blocking collectives: none -> 11.9 us  [on_device(): lax.all_to_all(grad_packed, 'mp', split_axis=1, concat_axis=0, tiled=True)]
    all_to_all x1, waiting for transfers between devices: 23.2 us -> 14.1 us  [on_device(): lax.all_to_all(grad_mine, 'dp', split_axis=0, concat_axis=0, tiled=True)]
  transfers between devices with their start and end apart: 8 -> 4, of which waited for: 8 -> 2; matrix products, arithmetic and copies ran while one was open for 14% -> 16% of each run, Pallas kernels for 0% -> 24%
where the time goes in v1:
time: 238 us
  Pallas kernels  68.8 us (29%)
  matrix products  54.5 us (23%)
  blocking collectives  33.5 us (14%)
  waiting for transfers between devices  24.7 us (10%)
  other arithmetic  21.6 us (9%)
  local copies, waits for them, and re-layouts  16.5 us (7%)
  between operations  14.1 us (6%)
  starting transfers between devices  4.06 us (2%)
    pallas_call x2, Pallas kernels, scatter_sum(): pl.pallas_call(functools.partial(scatter_sum_kernel, parts, count), out_s...  68.8 us
    dot_general x5, matrix products, contract_rows(): lax.dot_general(left, right, (((0,), (0,)), ((), ())), preferred_element_...  24.2 us
    all_to_all x1, blocking collectives, on_device(): lax.all_to_all(outgoing, 'dp', split_axis=0, concat_axis=0, tiled=True)  21.6 us
    unnamed x47, local copies, waits for them, and re-layouts  15.1 us
    all_to_all x1, waiting for transfers between devices, on_device(): lax.all_to_all(grad_mine, 'dp', split_axis=0, concat_axis=0, tiled=True)  14.1 us
    all_to_all x1, blocking collectives, on_device(): lax.all_to_all(grad_packed, 'mp', split_axis=1, concat_axis=0, tiled=True)  11.9 us
    all_gather x1, waiting for transfers between devices, on_device(): packed = lax.all_gather(arrived, 'mp', axis=1, tiled=True)  10.5 us
    dot_general x2, matrix products, contract_cols(): lax.dot_general(left, right, (((1,), (1,)), ((), ())), preferred_element_...  8.8 us
  transfers between devices with their start and end apart: 4, of which 2 were waited for; matrix products, arithmetic and copies ran while one was open for 16% of the time, Pallas kernels for 24%

profile of v1, /device:TPU:0, one launch (start us, length us, event | category | flops | bytes accessed | tf_op | source)
XLA Modules:
  0.0 237.8 jit_solution(5075425907688737821)
XLA Ops:
  7.2 3.6 %fusion.36 = f32[2048,128]{1,0:T(8,128)S(1)} fusion(bf16[2048,1024]{1,0:T(8,128)(2,1)} %param.10, bf16[1024,128]{1,0:T(8,128)(2,1)} %param.11), kind=kOutput, calls=%fused_computation.68 | convolution fusion | flops 536870912 | bytes 5505024 | tf_op jit(solution)/shard_map/dot_general | solution.py:175
  10.9 3.1 %fusion.16 = bf16[2048,128]{1,0:T(8,128)(2,1)S(1)} fusion(s32[2048]{0:T(1024)S(1)} %copy-done.17, f32[2048,128]{1,0:T(8,128)S(1)} %fusion.36), kind=kOutput, calls=%fused_computation.27 | convolution fusion | flops 1079508992 | bytes 1581056 | tf_op jit(solution)/shard_map/dot_general | solution.py:178
  14.1 21.6 %all_to_all.40 = bf16[8,256,128]{2,1,0:T(8,128)(2,1)S(1)} all-to-all(bf16[8,256,128]{2,1,0:T(8,128)(2,1)S(1)} %bitcast.34), channel_id=1, replica_groups=mesh['dp'=8,'mp'=4] {'dp'}, dimensions={0} | all-to-all | bytes 1048576 | tf_op jit(solution)/shard_map/all_to_all | solution.py:179
  35.7 1.0 copy.25
  37.0 6.6 %copy.19 = bf16[2048,1024]{0,1:T(8,128)(2,1)} copy(bf16[2048,1024]{1,0:T(8,128)(2,1)} %param.17) | data formatting | bytes 8388608 | tf_op args[7]
  43.5 4.5 %broadcast_multiply_fusion = bf16[2048,1024]{0,1:T(8,128)(2,1)} fusion(bf16[2048,1024]{0,1:T(8,128)(2,1)} %copy.19, bf16[2048]{0:T(1024)(128)(2,1)S(1)} %convert_element_type.60), kind=kLoop, calls=%fused_computation.30 | loop fusion | flops 2097152 | bytes 8392704 | tf_op jit(solution)/shard_map/mul | solution.py:188
  48.0 10.5 %all-gather.2.cloned.1.call-done = bf16[2048,512]{0,1:T(8,128)(2,1)} async-done(((bf16[2048,128]{0,1:T(8,128)(2,1)}), bf16[2048,512]{0,1:T(8,128)(2,1)}) %all-gather.2.cloned.1.call-update) | async-done | bytes 2097168 | tf_op jit(solution)/shard_map/all_gather | solution.py:180
  58.5 2.1 convert_reduce_fusion
  60.6 2.2 fusion.11
  62.8 2.6 %fusion.9 = (f32[2048,512]{0,1:T(8,128)}, bf16[2048,512]{0,1:T(8,128)(2,1)S(1)}) fusion(bf16[2048,512]{0,1:T(8,128)(2,1)S(1)} %copy-done.5, f32[2048]{0:T(1024)S(1)} %add_rsqrt_fusion.1, f32[2048]{0:T(1024)S(1)} %broadcast_multiply_fusion.2, f32[512]{0:T(512)S(1)} %copy-done.14), kind=kLoop, calls=%fused_computation.18 | loop fusion | flops 5242880 | bytes 8407040 | tf_op jit(solution)/shard_map/mul | solution.py:30
  65.4 2.5 %fusion.35 = (f32[2048]{0:T(1024)S(1)}, f32[2048,1024]{0,1:T(8,128)S(1)}) fusion(bf16[2048,512]{0,1:T(8,128)(2,1)S(1)} %get-tuple-element.23, bf16[512,1024]{1,0:T(8,128)(2,1)S(1)} %copy-done.16), kind=kOutput, calls=%fused_computation.67 | convolution fusion | flops 2149578752 | bytes 11542528 | tf_op jit(solution)/shard_map/dot_general | solution.py:183
  68.8 1.9 subtract_multiply_fusion
  70.7 4.9 %fusion.33 = f32[2048,1024]{1,0:T(8,128)S(1)} fusion(bf16[1024,1024]{1,0:T(8,128)(2,1)S(1)} %copy-done, f32[2048,1024]{0,1:T(8,128)S(1)} %subtract_multiply_fusion, f32[1024]{0:T(1024)S(1)} %copy-done.12), kind=kOutput, calls=%fused_computation.65 | convolution fusion | flops 4299161600 | bytes 18878464 | tf_op jit(solution)/shard_map/dot_general | solution.py:186
  76.6 7.3 %fusion.6 = bf16[2048,1024]{1,0:T(8,128)(2,1)S(1)} fusion(f32[2048,1024]{1,0:T(8,128)S(1)} %fusion.33, bf16[2048,1024]{0,1:T(8,128)(2,1)S(1)} %copy-done.6, bf16[1024,1024]{1,0:T(8,128)(2,1)S(1)} %copy-done.15), kind=kOutput, calls=%fused_computation.8 | convolution fusion | flops 4315938816 | bytes 18874368 | tf_op jit(solution)/shard_map/dot_general | solution.py:189
  83.9 2.0 copy-done.20
  85.9 6.1 %convolution_convert_fusion = bf16[2048,1024]{0,1:T(8,128)(2,1)} fusion(bf16[2048,1024]{1,0:T(8,128)(2,1)S(1)} %fusion.6, bf16[1024,1024]{1,0:T(8,128)(2,1)S(1)} %copy-done), kind=kOutput, calls=%fused_computation.24 | convolution fusion | flops 4297064448 | bytes 10485760 | tf_op jit(solution)/shard_map/dot_general | solution.py:47
  92.3 9.2 %convolution_convert_fusion.1.refs_0_ = bf16[1024,1024]{1,0:T(8,128)(2,1)S(1)} fusion(bf16[2048,1024]{1,0:T(8,128)(2,1)} %copy-done.20, f32[2048,1024]{0,1:T(8,128)} %copy-done.4, f32[1024]{0:T(1024)S(1)} %copy-done.12), kind=kOutput, calls=%fused_computation.31 | convolution fusion | flops 4300210176 | bytes 14684160 | tf_op jit(solution)/shard_map/dot_general | solution.py:41
  102.3 5.4 %fusion.17.refs_1_ = bf16[1024,1024]{1,0:T(8,128)(2,1)S(1)} fusion(bf16[2048,1024]{0,1:T(8,128)(2,1)S(1)} %copy-done.7, f32[2048,1024]{1,0:T(8,128)S(1)} %copy-done.19), kind=kOutput, calls=%fused_computation.32 | convolution fusion | flops 4306501632 | bytes 14680064 | tf_op jit(solution)/shard_map/dot_general | solution.py:41
  107.6 57.3 %scatter_sum.2 = (f32[128,1024]{1,0:T(8,128)S(1)}, f32[128,1024]{1,0:T(8,128)S(1)}) custom-call(bf16[1024,1024]{1,0:T(8,128)(2,1)S(1)} %convolution_convert_fusion.1.refs_0_, bf16[1024,1024]{1,0:T(8,128)(2,1)S(1)} %fusion.17.refs_1_), custom_call_target="tpu_custom_call" | custom-call | flops 16777216000 | bytes 167772160 | tf_op jit(solution)/shard_map/scatter_sum/pallas_call | solution.py:144
  165.0 1.5 convert_element_type.66
  166.5 1.9 multiply_reduce_fusion.2
  168.4 2.4 %add_convert_fusion = bf16[512,1024]{0,1:T(8,128)(2,1)S(1)} fusion(f32[2048,1024]{0,1:T(8,128)} %copy-done.4, s32[]{:T(128)S(6)} %select_n.2, f32[512,1024]{0,1:T(8,128)S(1)} %convert_element_type.66, f32[512]{0:T(512)S(1)} %get-tuple-element.27, f32[512]{0:T(512)S(1)} %get-tuple-element.28, f32[1024]{0:T(1024)S(1)} %copy-done.12, f32[512]{0:T(512)S(1)} %dynamic-slice.7, ...), kind=kLoop, calls=%fused_computation.28 | loop fusion | flops 4194304 | bytes 6301700 | tf_op jit(solution)/shard_map/convert_element_type | solution.py:206
  170.9 1.0 copy-done.11
  171.9 2.8 %convolution_convert_fusion.2 = bf16[512,1024]{1,0:T(8,128)(2,1)} fusion(bf16[512,1024]{0,1:T(8,128)(2,1)S(1)} %add_convert_fusion, bf16[2048,512]{0,1:T(8,128)(2,1)} %copy-done.8, s32[]{:T(128)S(6)} %select_n.2), kind=kOutput, calls=%fused_computation.35 | convolution fusion | flops 537395200 | bytes 2621444 | tf_op jit(solution)/shard_map/dot_general | solution.py:41
  174.7 2.7 %fusion.34 = (f32[512]{0:T(512)S(1)}, f32[512]{0:T(512)S(1)}, f32[512,512]{0,1:T(8,128)S(1)}) fusion(f32[2048,512]{0,1:T(8,128)} %get-tuple-element.22, s32[]{:T(128)S(6)} %select_n.2, f32[512]{0:T(512)S(1)} %copy-done.14, bf16[512,1024]{1,0:T(8,128)(2,1)} %param.13, bf16[512,1024]{0,1:T(8,128)(2,1)} %copy-done.11), kind=kOutput, calls=%fused_computation.66 | convolution fusion | flops 537918464 | bytes 4200452 | tf_op jit(solution)/shard_map/dot_general | solution.py:47
  177.4 1.6 multiply_convert_fusion.6
  179.3 11.9 %all_to_all.41 = bf16[512,4,128]{2,0,1:T(8,128)(2,1)} all-to-all(bf16[512,4,128]{2,0,1:T(8,128)(2,1)S(1)} %copy.21), channel_id=1, replica_groups=mesh['dp'=8,'mp'=4] {'mp'}, dimensions={1} | all-to-all | bytes 1048576 | tf_op jit(solution)/shard_map/all_to_all | solution.py:220
  191.2 3.8 %all-to-all-start.2 = ((bf16[8,256,128]{2,1,0:T(8,128)(2,1)}), bf16[8,256,128]{2,1,0:T(8,128)(2,1)S(1)}, u32[]{:S(2)}, u32[]{:S(2)}) async-start(bf16[8,256,128]{2,1,0:T(8,128)(2,1)} %bitcast.4), calls=%async_computation.3 | async-start | bytes 1048576 | tf_op jit(solution)/shard_map/all_to_all | solution.py:221
  194.9 14.1 %all-to-all-done.2 = bf16[8,256,128]{2,1,0:T(8,128)(2,1)S(1)} async-done(((bf16[8,256,128]{2,1,0:T(8,128)(2,1)}), bf16[8,256,128]{2,1,0:T(8,128)(2,1)S(1)}, u32[]{:S(2)}, u32[]{:S(2)}) %all-to-all-start.2) | async-done | bytes 524320 | tf_op jit(solution)/shard_map/all_to_all | solution.py:221
  209.1 5.0 %fusion.15.clone.4 = bf16[2048,128]{1,0:T(8,128)(2,1)S(1)} fusion(bf16[2048,128]{1,0:T(8,128)(2,1)S(1)} %bitcast.33, s32[2048]{0:T(1024)S(1)} %copy-done.17, f32[2048,128]{1,0:T(8,128)S(1)} %copy-done.10), kind=kOutput, calls=%fused_computation.26.clone.clone.clone.1 | convolution fusion | flops 1080557568 | bytes 2105344 | tf_op jit(solution)/shard_map/dot_general | solution.py:41
  214.1 1.8 fusion.18.refs_0_
  216.9 11.5 %scatter_sum.3 = (f32[128,128]{1,0:T(8,128)S(1)}, f32[64,256]{1,0:T(8,128)S(1)}) custom-call(bf16[1024,128]{1,0:T(8,128)(2,1)S(1)} %fusion.18.refs_0_, bf16[512,256]{1,0:T(8,128)(2,1)S(1)} %copy-done.2), custom_call_target="tpu_custom_call" | custom-call | flops 2097152000 | bytes 20971520 | tf_op jit(solution)/shard_map/scatter_sum/pallas_call | solution.py:144
  (64 shorter events, 7.3 us)
Async XLA Ops:
  7.2 63.5 %copy-start = (bf16[1024,1024]{1,0:T(8,128)(2,1)S(1)}, bf16[1024,1024]{1,0:T(8,128)(2,1)}, u32[]{:S(2)}) copy-start(bf16[1024,1024]{1,0:T(8,128)(2,1)} %param.15) | copy-start | bytes 6291460
  7.2 3.7 %copy-start.17 = (s32[2048]{0:T(1024)S(1)}, s32[2048]{0:T(1024)}, u32[]{:S(2)}) copy-start(s32[2048]{0:T(1024)} %param.18) | copy-start | bytes 24580
  7.2 51.3 %all-gather.2.cloned.1.call-start = ((), (), s32[]{:S(2)}) async-start(), calls=%async_computation.5 | async-start | bytes 2621440 | tf_op jit(solution)/shard_map/all_gather | solution.py:180
  10.9 3.2 %copy-start.9 = (f32[2048,128]{1,0:T(8,128)}, f32[2048,128]{1,0:T(8,128)S(1)}, u32[]{:S(2)}) copy-start(f32[2048,128]{1,0:T(8,128)S(1)} %fusion.36) | copy-start | bytes 3145732
  10.9 26.0 %copy-start.13 = (s32[2048]{0:T(1024)S(1)}, s32[2048]{0:T(1024)}, u32[]{:S(2)}) copy-start(s32[2048]{0:T(1024)} %param.19) | copy-start | bytes 24580
  36.7 128.2 %reduce-scatter.3.cloned.1.call-start = ((), (), s32[]{:S(2)}) async-start(), calls=%async_computation.6 | async-start | bytes 5242880 | tf_op jit(solution)/shard_map/reduce_scatter | solution.py:196
  48.0 14.8 %copy-start.14 = (f32[512]{0:T(512)S(1)}, f32[512]{0:T(512)}, u32[]{:S(2)}) copy-start(f32[512]{0:T(512)} %param.12) | copy-start | bytes 6148
  58.5 4.3 %copy-start.5 = (bf16[2048,512]{0,1:T(8,128)(2,1)S(1)}, bf16[2048,512]{0,1:T(8,128)(2,1)}, u32[]{:S(2)}) copy-start(bf16[2048,512]{0,1:T(8,128)(2,1)} %all-gather.2.cloned.1.call-done) | copy-start | bytes 6291460
  62.8 2.6 %copy-start.16 = (bf16[512,1024]{1,0:T(8,128)(2,1)S(1)}, bf16[512,1024]{1,0:T(8,128)(2,1)}, u32[]{:S(2)}) copy-start(bf16[512,1024]{1,0:T(8,128)(2,1)} %param.13) | copy-start | bytes 3145732
  65.4 2.5 %copy-start.8 = (bf16[2048,512]{0,1:T(8,128)(2,1)}, bf16[2048,512]{0,1:T(8,128)(2,1)S(1)}, u32[]{:S(2)}) copy-start(bf16[2048,512]{0,1:T(8,128)(2,1)S(1)} %get-tuple-element.23) | copy-start | bytes 6291460
  68.8 1.9 copy-start.12
  70.7 4.9 %copy-start.4 = (f32[2048,1024]{0,1:T(8,128)}, f32[2048,1024]{0,1:T(8,128)S(1)}, u32[]{:S(2)}) copy-start(f32[2048,1024]{0,1:T(8,128)S(1)} %subtract_multiply_fusion) | copy-start | bytes 25165828
  70.7 5.2 %copy-start.6 = (bf16[2048,1024]{0,1:T(8,128)(2,1)S(1)}, bf16[2048,1024]{0,1:T(8,128)(2,1)}, u32[]{:S(2)}) copy-start(bf16[2048,1024]{0,1:T(8,128)(2,1)} %broadcast_multiply_fusion) | copy-start | bytes 12582916
  70.7 5.9 %copy-start.15 = (bf16[1024,1024]{1,0:T(8,128)(2,1)S(1)}, bf16[1024,1024]{1,0:T(8,128)(2,1)}, u32[]{:S(2)}) copy-start(bf16[1024,1024]{1,0:T(8,128)(2,1)} %param.16) | copy-start | bytes 6291460
  76.6 7.3 %copy-start.18 = (f32[2048,1024]{1,0:T(8,128)}, f32[2048,1024]{1,0:T(8,128)S(1)}, u32[]{:S(2)}) copy-start(f32[2048,1024]{1,0:T(8,128)S(1)} %fusion.33) | copy-start | bytes 25165828
  83.9 2.0 copy-start.20
  92.0 123.9 %reduce-scatter.5.cloned.1.call-start = ((), (), s32[]{:S(2)}) async-start(), calls=%async_computation.7 | async-start | bytes 1310720 | tf_op jit(solution)/shard_map/reduce_scatter | solution.py:217
  92.3 9.3 %copy-start.7 = (bf16[2048,1024]{0,1:T(8,128)(2,1)S(1)}, bf16[2048,1024]{0,1:T(8,128)(2,1)}, u32[]{:S(2)}) copy-start(bf16[2048,1024]{0,1:T(8,128)(2,1)} %broadcast_multiply_fusion) | copy-start | bytes 12582916
  92.3 10.0 %copy-start.19 = (f32[2048,1024]{1,0:T(8,128)S(1)}, f32[2048,1024]{1,0:T(8,128)}, u32[]{:S(2)}) copy-start(f32[2048,1024]{1,0:T(8,128)} %copy-done.18) | copy-start | bytes 25165828
  170.9 1.0 copy-start.11
  174.7 34.4 %copy-start.10 = (f32[2048,128]{1,0:T(8,128)S(1)}, f32[2048,128]{1,0:T(8,128)}, u32[]{:S(2)}) copy-start(f32[2048,128]{1,0:T(8,128)} %copy-done.9) | copy-start | bytes 3145732
  191.2 17.9 %all-to-all-start.2 = ((bf16[8,256,128]{2,1,0:T(8,128)(2,1)}), bf16[8,256,128]{2,1,0:T(8,128)(2,1)S(1)}, u32[]{:S(2)}, u32[]{:S(2)}) async-start(bf16[8,256,128]{2,1,0:T(8,128)(2,1)} %bitcast.4), calls=%async_computation.3 | async-start | bytes 1048576 | tf_op jit(solution)/shard_map/all_to_all | solution.py:221
  209.1 5.0 %copy-start.3 = (bf16[2048,1024]{1,0:T(8,128)(2,1)S(1)}, bf16[2048,1024]{1,0:T(8,128)(2,1)}, u32[]{:S(2)}) copy-start(bf16[2048,1024]{1,0:T(8,128)(2,1)} %param.10) | copy-start | bytes 12582916
  214.1 17.1 %copy-start.1 = (bf16[1024,1024]{1,0:T(8,128)(2,1)S(1)}, bf16[1024,1024]{1,0:T(8,128)(2,1)}, u32[]{:S(2)}) copy-start(bf16[1024,1024]{1,0:T(8,128)(2,1)} %param.15) | copy-start | bytes 6291460
  216.0 1.0 copy-start.2
Sparse Core Ops, SparseCore 0:
  36.8 21.5 all-gather.1
  92.2 44.3 reduce-scatter.2
  174.8 23.1 reduce-scatter.4

commit v2 on v1

--- a/solution.py
+++ b/solution.py
@@ -134,6 +134,275 @@
         copy.wait_send()
 
 
+def start_copy(src, dst, send_sem, recv_sem, axis, index):
+    copy = pltpu.make_async_remote_copy(
+        src_ref=src,
+        dst_ref=dst,
+        send_sem=send_sem,
+        recv_sem=recv_sem,
+        device_id={axis: index},
+        device_id_type=pl.DeviceIdType.MESH,
+    )
+    copy.start()
+    return copy
+
+
+def greet(peers):
+    barrier = pltpu.get_barrier_semaphore()
+    for axis, index in peers:
+        pl.semaphore_signal(
+            barrier, inc=1, device_id={axis: index}, device_id_type=pl.DeviceIdType.MESH
+        )
+    pl.semaphore_wait(barrier, len(peers))
+
+
+def block_of(index, size):
+    return pl.ds(pl.multiple_of(index * size, size), size)
+
+
+def forward_kernel(
+    parts, shards, source, packed, arrived, dp_send, dp_recv, near_send, near_recv,
+    far_send, far_recv, on_send, on_recv, local
+):
+    rows, width = source.shape[0] // parts, source.shape[1]
+    d = lax.axis_index("dp")
+    m = lax.axis_index("mp")
+    near = m + 1 - 2 * lax.rem(m, 2)
+    fars = shards // 2
+    greet(
+        [("dp", lax.rem(d + o, parts)) for o in range(1, parts)]
+        + [("mp", near)]
+        + [("mp", lax.rem(m + 2 * j, shards)) for j in range(1, fars)]
+    )
+    exchanged, passed, kept = [], [], []
+    spans, far_copies = [], []
+    for o in range(1, parts):
+        target = lax.rem(d + o, parts)
+        exchanged.append(
+            start_copy(
+                source.at[block_of(target, rows)],
+                arrived.at[block_of(d, rows)],
+                dp_send.at[o],
+                dp_recv.at[o],
+                "dp",
+                target,
+            )
+        )
+
+    def hand_on(o):
+        for j in range(1, fars):
+            far_copies[o][j - 1].wait_recv()
+            col = block_of(lax.rem(m - 2 * j + shards, shards), width)
+            piece = packed.at[spans[o], col]
+            passed.append(
+                start_copy(piece, piece, on_send.at[o, j], on_recv.at[o, j], "mp", near)
+            )
+
+    lag = 2
+    nears = []
+    for o in range(parts):
+        span = block_of(lax.rem(d - o + parts, parts), rows)
+        spans.append(span)
+        if o:
+            exchanged[o - 1].wait_recv()
+        block = arrived.at[span] if o else source.at[span]
+        mine = packed.at[span, block_of(m, width)]
+        far_copies.append(
+            [
+                start_copy(
+                    block, mine, far_send.at[o, j], far_recv.at[o, j], "mp",
+                    lax.rem(m + 2 * j, shards),
+                )
+                for j in range(1, fars)
+            ]
+        )
+        nears.append(start_copy(block, mine, near_send.at[o], near_recv.at[o], "mp", near))
+        keep = pltpu.make_async_copy(block, mine, local.at[o])
+        keep.start()
+        kept.append(keep)
+        if o >= lag:
+            hand_on(o - lag)
+    for o in range(parts - lag, parts):
+        hand_on(o)
+    for copy in nears + passed:
+        copy.wait_recv()
+    for copy in kept:
+        copy.wait()
+    for copy in exchanged + nears + passed + [c for group in far_copies for c in group]:
+        copy.wait_send()
+
+
+def forward_exchange(source, collective_id):
+    parts, shards = lax.axis_size("dp"), lax.axis_size("mp")
+    rows, width = source.shape
+    fars = max(shards // 2, 1)
+    return pl.pallas_call(
+        functools.partial(forward_kernel, parts, shards),
+        out_shape=jax.ShapeDtypeStruct((rows, width * shards), source.dtype),
+        in_specs=[pl.BlockSpec(memory_space=pltpu.VMEM)],
+        out_specs=pl.BlockSpec(memory_space=pltpu.VMEM),
+        scratch_shapes=[pltpu.VMEM((rows, width), source.dtype)]
+        + [pltpu.SemaphoreType.DMA((parts,))] * 4
+        + [pltpu.SemaphoreType.DMA((parts, fars))] * 4
+        + [pltpu.SemaphoreType.DMA((parts,))],
+        compiler_params=pltpu.CompilerParams(
+            collective_id=collective_id, has_side_effects=True, vmem_limit_bytes=VMEM_LIMIT
+        ),
+        name="forward_exchange",
+    )(source)
+
+
+def backward_kernel(
+    parts, shards, grad, term, back, total_out, middle, first_in, staged, second_in,
+    mp_send, mp_recv, dp_send, dp_recv, send_one, recv_one, send_two, recv_two, local
+):
+    share = grad.shape[0]
+    rows, width = back.shape[0] // parts, back.shape[1]
+    out_rows = total_out.shape[0]
+    half = parts // 2
+    d = lax.axis_index("dp")
+    m = lax.axis_index("mp")
+    parity = lax.rem(d, 2)
+    place = d // 2
+    partner = d + 1 - 2 * parity
+    order = list(range(1, half)) + [0]
+    greet(
+        [("dp", lax.rem(d + o, parts)) for o in range(1, parts)]
+        + [("mp", lax.rem(m + o, shards)) for o in range(1, shards)]
+    )
+    columns = []
+    for o in range(1, shards):
+        peer = lax.rem(m + o, shards)
+        columns.append(
+            start_copy(
+                grad.at[:, block_of(peer, width)],
+                middle.at[block_of(m, share)],
+                mp_send.at[o],
+                mp_recv.at[o],
+                "mp",
+                peer,
+            )
+        )
+    own_column = pltpu.make_async_copy(
+        grad.at[:, block_of(m, width)], middle.at[block_of(m, share)], local.at[0]
+    )
+    own_column.start()
+
+    def pair(k):
+        target = lax.rem(place + k, half)
+        return start_copy(
+            term.at[block_of(2 * target + 1 - parity, out_rows)],
+            first_in.at[k],
+            send_one.at[k],
+            recv_one.at[k],
+            "dp",
+            partner,
+        )
+
+    ones = {order[0]: pair(order[0])}
+    for copy in columns:
+        copy.wait_recv()
+    own_column.wait()
+    blocks = []
+    for o in range(1, parts):
+        target = lax.rem(d + o, parts)
+        blocks.append(
+            start_copy(
+                middle.at[block_of(target, rows)],
+                back.at[block_of(d, rows)],
+                dp_send.at[o],
+                dp_recv.at[o],
+                "dp",
+                target,
+            )
+        )
+    own_block = pltpu.make_async_copy(
+        middle.at[block_of(d, rows)], back.at[block_of(d, rows)], local.at[1]
+    )
+    own_block.start()
+    for k in order[1:]:
+        ones[k] = pair(k)
+
+    def each_tile(body):
+        def step(i, carry):
+            body(block_of(i, 16), i)
+            return carry
+
+        lax.fori_loop(0, out_rows // 16, step, 0)
+
+    twos = []
+    for k in order:
+        target = lax.rem(place + k, half)
+        base = (2 * target + parity) * out_rows
+        ones[k].wait_recv()
+
+        def add(tile, step, k=k, base=base):
+            mine = term[pl.ds(pl.multiple_of(base + step * 16, 16), 16), :]
+            total = mine.astype(jnp.float32) + first_in[k, tile, :].astype(jnp.float32)
+            if k:
+                staged[k, tile, :] = total.astype(jnp.bfloat16)
+            else:
+                total_out[tile, :] = total
+
+        each_tile(add)
+        if k:
+            twos.append(
+                start_copy(
+                    staged.at[k],
+                    second_in.at[k],
+                    send_two.at[k],
+                    recv_two.at[k],
+                    "dp",
+                    2 * target + parity,
+                )
+            )
+    for copy in twos:
+        copy.wait_recv()
+
+    def gather(tile, step):
+        total = total_out[tile, :]
+        for k in range(1, half):
+            total = total + second_in[k, tile, :].astype(jnp.float32)
+        total_out[tile, :] = total
+
+    each_tile(gather)
+    for copy in blocks:
+        copy.wait_recv()
+    own_block.wait()
+    for copy in columns + blocks + list(ones.values()) + twos:
+        copy.wait_send()
+
+
+def backward_exchange(grad, term, collective_id):
+    parts, shards = lax.axis_size("dp"), lax.axis_size("mp")
+    half = parts // 2
+    share, channels = grad.shape
+    back = (share * shards, channels // shards)
+    block = (term.shape[0] // parts, term.shape[1])
+    slots = pltpu.VMEM((half,) + block, jnp.bfloat16)
+    return pl.pallas_call(
+        functools.partial(backward_kernel, parts, shards),
+        out_shape=[
+            jax.ShapeDtypeStruct(back, grad.dtype),
+            jax.ShapeDtypeStruct(block, jnp.float32),
+        ],
+        in_specs=[pl.BlockSpec(memory_space=pltpu.VMEM)] * 2,
+        out_specs=[pl.BlockSpec(memory_space=pltpu.VMEM)] * 2,
+        scratch_shapes=[pltpu.VMEM(back, grad.dtype), slots, slots, slots]
+        + [pltpu.SemaphoreType.DMA((shards,))] * 2
+        + [pltpu.SemaphoreType.DMA((parts,))] * 2
+        + [pltpu.SemaphoreType.DMA((half,))] * 4
+        + [pltpu.SemaphoreType.DMA((2,))],
+        compiler_params=pltpu.CompilerParams(
+            collective_id=collective_id, has_side_effects=True, vmem_limit_bytes=VMEM_LIMIT
+        ),
+        cost_estimate=pl.CostEstimate(
+            flops=term.size * 8000, bytes_accessed=term.size * 80, transcendentals=0
+        ),
+        name="backward_exchange",
+    )(grad, term)
+
+
 def scatter_sum(terms, collective_id):
     parts = lax.axis_size("dp")
     half = parts // 2
@@ -176,19 +445,18 @@
     features = gelu_exact(pre_act).astype(jnp.bfloat16)
     choose = (send_index[:, None] == jnp.arange(frames, dtype=send_index.dtype)).astype(jnp.bfloat16)
     outgoing = jnp.dot(choose, features, preferred_element_type=jnp.float32).astype(jnp.bfloat16)
-    arrived = lax.all_to_all(outgoing, "dp", split_axis=0, concat_axis=0, tiled=True)
-    packed = lax.all_gather(arrived, "mp", axis=1, tiled=True)
+    packed = forward_exchange(outgoing, 3)
     feat_norm, feat_inv = normalize(packed.astype(jnp.float32))
     feat_ln = (feat_norm * feature_gain).astype(jnp.bfloat16)
     hidden = jnp.dot(feat_ln, proj_weight, preferred_element_type=jnp.float32)
     hid_norm, hid_inv = normalize(hidden)
     hid_ln = (hid_norm * block_gain).astype(jnp.bfloat16)
     upward = jnp.dot(hid_ln, w_in, preferred_element_type=jnp.float32)
-    active = gelu_exact(upward).astype(jnp.bfloat16)
-    masked_cot = cotangent * slot_valid.astype(jnp.bfloat16)[:, None]
-    grad_active = jnp.dot(masked_cot, w_out, preferred_element_type=jnp.float32)
+    valid = slot_valid.astype(jnp.float32)[:, None]
+    active = (valid * gelu_exact(upward)).astype(jnp.bfloat16)
+    grad_active = valid * jnp.dot(cotangent, w_out, preferred_element_type=jnp.float32)
     grad_upward = (grad_active * gelu_slope(upward)).astype(jnp.bfloat16)
-    out_term = contract_rows(masked_cot, active)
+    out_term = contract_rows(cotangent, active)
     in_term = contract_rows(hid_ln, grad_upward)
     partial_value = contract_cols(grad_upward, w_in)
     share_rows = frames // shards
@@ -196,11 +464,12 @@
     share_normed = lax.psum_scatter(
         partial_value.astype(jnp.bfloat16), "mp", scatter_dimension=0, tiled=True
     ).astype(jnp.float32)
-    in_grad, out_grad = scatter_sum(
-        [in_term.astype(jnp.bfloat16), out_term.astype(jnp.bfloat16)], 1
-    )
-    share_normed, in_grad, out_grad = lax.optimization_barrier((share_normed, in_grad, out_grad))
-    share_cot = lax.dynamic_slice_in_dim(masked_cot, first_row, share_rows, 0).astype(jnp.float32)
+    in_term = in_term.astype(jnp.bfloat16)
+    (out_grad,) = scatter_sum([out_term.astype(jnp.bfloat16)], 1)
+    share_normed, in_term, out_grad = lax.optimization_barrier((share_normed, in_term, out_grad))
+    share_cot = lax.dynamic_slice_in_dim(valid, first_row, share_rows, 0) * (
+        lax.dynamic_slice_in_dim(cotangent, first_row, share_rows, 0).astype(jnp.float32)
+    )
     share_norm = lax.dynamic_slice_in_dim(hid_norm, first_row, share_rows, 0)
     share_inv = lax.dynamic_slice_in_dim(hid_inv, first_row, share_rows, 0)
     share_grad = (share_cot + norm_back(share_normed, share_norm, share_inv, block_gain)).astype(
@@ -217,8 +486,7 @@
     proj_part = lax.psum_scatter(
         proj_term.astype(jnp.bfloat16), "mp", scatter_dimension=1, tiled=True
     )
-    grad_mine = lax.all_to_all(grad_packed, "mp", split_axis=1, concat_axis=0, tiled=True)
-    returned = lax.all_to_all(grad_mine, "dp", split_axis=0, concat_axis=0, tiled=True)
+    returned, in_grad = backward_exchange(grad_packed, in_term, 4)
     grad_features = contract_rows(choose, returned)
     grad_pre = (grad_features * gelu_slope(pre_act)).astype(jnp.bfloat16)
     conv_term = contract_rows(conv_in, grad_pre)

time: 238 us -> 217 us (0.912)
  Pallas kernels: 68.8 us -> 117 us
  blocking collectives: 33.5 us -> 0 us
  waiting for transfers between devices: 24.7 us -> 0.07 us
  other arithmetic: 21.6 us -> 14.9 us
  local copies, waits for them, and re-layouts: 16.5 us -> 11.6 us
  starting transfers between devices: 4.06 us -> 0.3 us
  matrix products: 54.5 us -> 57.7 us
    pallas_call x0 -> x2, Pallas kernels: none -> 64.8 us  [the longest x1 39.8 us: backward_exchange(): pl.pallas_call(functools.partial(backward_kernel, parts, shards), out_sha...]
    all_to_all x2 -> x0, blocking collectives: 33.5 us -> none  [the longest x1 21.6 us: on_device(): lax.all_to_all(outgoing, 'dp', split_axis=0, concat_axis=0, tiled=True)]
    pallas_call x2, Pallas kernels: 68.8 us -> 52.7 us  [scatter_sum(): pl.pallas_call(functools.partial(scatter_sum_kernel, parts, count), out_s...]
    all_to_all x1 -> x0, waiting for transfers between devices: 14.1 us -> none  [on_device(): lax.all_to_all(grad_mine, 'dp', split_axis=0, concat_axis=0, tiled=True)]
    all_gather x1 -> x0, waiting for transfers between devices: 10.5 us -> none  [on_device(): packed = lax.all_gather(arrived, 'mp', axis=1, tiled=True)]
    unnamed x47 -> x43, local copies, waits for them, and re-layouts: 15.1 us -> 10.1 us
    mul x1 -> x0, other arithmetic: 4.46 us -> none  [on_device(): masked_cot = cotangent * slot_valid.astype(jnp.bfloat16)[:, None]]
    all_to_all x1 -> x0, starting transfers between devices: 3.75 us -> none  [on_device(): lax.all_to_all(grad_mine, 'dp', split_axis=0, concat_axis=0, tiled=True)]
  transfers between devices with their start and end apart: 4 -> 2, of which waited for: 2 -> 0; matrix products, arithmetic and copies ran while one was open for 16% -> 14% of each run, Pallas kernels for 24% -> 35%
where the time goes in v2:
time: 217 us; the launch traced here: 216 us
  Pallas kernels  117 us (54%)
  matrix products  57.7 us (27%)
  other arithmetic  14.9 us (7%)
  between operations  14.5 us (7%)
  local copies, waits for them, and re-layouts  11.6 us (5%)
    pallas_call x2, Pallas kernels, scatter_sum(): pl.pallas_call(functools.partial(scatter_sum_kernel, parts, count), out_s...  52.7 us
    pallas_call x1, Pallas kernels, backward_exchange(): pl.pallas_call(functools.partial(backward_kernel, parts, shards), out_sha...  39.8 us
    dot_general x5, matrix products, contract_rows(): lax.dot_general(left, right, (((0,), (0,)), ((), ())), preferred_element_...  26.6 us
    pallas_call x1, Pallas kernels, forward_exchange(): pl.pallas_call(functools.partial(forward_kernel, parts, shards), out_shap...  25 us
    unnamed x43, local copies, waits for them, and re-layouts  10.1 us
    dot_general x2, matrix products, contract_cols(): lax.dot_general(left, right, (((1,), (1,)), ((), ())), preferred_element_...  8.85 us
    dot_general x1, matrix products, on_device(): jnp.dot(cotangent, w_out, preferred_element_type=jnp.float32)  8.14 us
    dot_general x1, matrix products, on_device(): upward = jnp.dot(hid_ln, w_in, preferred_element_type=jnp.float32)  4.91 us
  transfers between devices with their start and end apart: 2, of which 0 were waited for; matrix products, arithmetic and copies ran while one was open for 14% of the time, Pallas kernels for 35%

profile of v2, /device:TPU:0, one launch (start us, length us, event | category | flops | bytes accessed | tf_op | source)
XLA Modules:
  0.0 216.4 jit_solution(2606716613056662363)
XLA Ops:
  7.2 0.8 convert_element_type.62
  8.1 3.5 %fusion.36 = f32[2048,128]{1,0:T(8,128)S(1)} fusion(bf16[2048,1024]{1,0:T(8,128)(2,1)} %param.10, bf16[1024,128]{1,0:T(8,128)(2,1)} %param.11), kind=kOutput, calls=%fused_computation.69 | convolution fusion | flops 536870912 | bytes 5505024 | tf_op jit(solution)/shard_map/dot_general | solution.py:444
  11.6 1.0 copy-done.7
  12.6 3.1 %fusion.17.source = bf16[2048,128]{1,0:T(8,128)(2,1)S(1)} fusion(s32[2048]{0:T(1024)S(1)} %copy-done.15, f32[2048,128]{1,0:T(8,128)S(1)} %fusion.36), kind=kOutput, calls=%fused_computation.28 | convolution fusion | flops 1079508992 | bytes 1581056 | tf_op jit(solution)/shard_map/dot_general | solution.py:447
  15.7 25.0 %forward_exchange.1 = bf16[2048,512]{1,0:T(8,128)(2,1)S(1)} custom-call(bf16[2048,128]{1,0:T(8,128)(2,1)S(1)} %fusion.17.source), custom_call_target="tpu_custom_call" | custom-call | tf_op jit(solution)/shard_map/forward_exchange/pallas_call | solution.py:239
  41.2 1.0 fusion.11
  42.2 2.6 %fusion.9 = (f32[2048,512]{1,0:T(8,128)}, bf16[2048,512]{1,0:T(8,128)(2,1)S(1)}) fusion(bf16[2048,512]{1,0:T(8,128)(2,1)S(1)} %forward_exchange.1, f32[2048]{0:T(1024)S(1)} %add_rsqrt_fusion.1, f32[2048]{0:T(1024)S(1)} %broadcast_multiply_fusion.1, f32[512]{0:T(512)S(1)} %copy-done.12), kind=kLoop, calls=%fused_computation.18 | loop fusion | flops 5242880 | bytes 8407040 | tf_op jit(solution)/shard_map/mul | solution.py:30
  44.8 2.5 %fusion.35 = (f32[2048]{0:T(1024)S(1)}, f32[2048,1024]{0,1:T(8,128)S(1)}) fusion(bf16[2048,512]{1,0:T(8,128)(2,1)S(1)} %get-tuple-element.23, bf16[512,1024]{1,0:T(8,128)(2,1)S(1)} %copy-done.14), kind=kOutput, calls=%fused_computation.68 | convolution fusion | flops 2149578752 | bytes 11542528 | tf_op jit(solution)/shard_map/dot_general | solution.py:451
  47.3 0.9 multiply_reduce_fusion
  48.2 1.9 subtract_multiply_fusion
  50.1 4.9 %fusion.33 = f32[2048,1024]{1,0:T(8,128)S(1)} fusion(bf16[1024,1024]{1,0:T(8,128)(2,1)S(1)} %copy-done, f32[2048,1024]{0,1:T(8,128)S(1)} %subtract_multiply_fusion, f32[1024]{0:T(1024)S(1)} %copy-done.11), kind=kOutput, calls=%fused_computation.66 | convolution fusion | flops 4299161600 | bytes 18878464 | tf_op jit(solution)/shard_map/dot_general | solution.py:454
  56.0 8.1 %fusion.6 = bf16[2048,1024]{1,0:T(8,128)(2,1)S(1)} fusion(f32[2048,1024]{1,0:T(8,128)S(1)} %fusion.33, bf16[2048,1024]{1,0:T(8,128)(2,1)S(1)} %copy-done.10, bf16[1024,1024]{1,0:T(8,128)(2,1)S(1)} %copy-done.13, f32[2048]{0:T(1024)S(1)} %convert_element_type.62), kind=kOutput, calls=%fused_computation.8 | convolution fusion | flops 4318035968 | bytes 18882560 | tf_op jit(solution)/shard_map/dot_general | solution.py:457
  64.1 1.9 copy-done.17
  66.1 6.1 %convolution_convert_fusion = bf16[2048,1024]{0,1:T(8,128)(2,1)} fusion(bf16[2048,1024]{1,0:T(8,128)(2,1)S(1)} %fusion.6, bf16[1024,1024]{1,0:T(8,128)(2,1)S(1)} %copy-done), kind=kOutput, calls=%fused_computation.25 | convolution fusion | flops 4297064448 | bytes 10485760 | tf_op jit(solution)/shard_map/dot_general | solution.py:47
  72.7 1.3 constant_dynamic-slice_fusion
  74.0 1.3 copy.23
  75.4 8.9 %convert_bitcast_fusion.refs_0_ = bf16[1024,1024]{1,0:T(8,128)(2,1)S(1)} fusion(bf16[2048,1024]{1,0:T(8,128)(2,1)} %param.17, f32[2048,1024]{1,0:T(8,128)} %copy-done.16, f32[2048]{0:T(1024)S(1)} %convert_element_type.62), kind=kOutput, calls=%fused_computation.31 | convolution fusion | flops 4308598784 | bytes 14688256 | tf_op jit(solution)/shard_map/dot_general | solution.py:41
  84.3 35.4 %scatter_sum.2 = f32[128,1024]{1,0:T(8,128)S(1)} custom-call(bf16[1024,1024]{1,0:T(8,128)(2,1)S(1)} %convert_bitcast_fusion.refs_0_), custom_call_target="tpu_custom_call" | custom-call | flops 8388608000 | bytes 83886080 | tf_op jit(solution)/shard_map/scatter_sum/pallas_call | solution.py:413
  119.8 8.2 %convolution_convert_fusion.1.term = bf16[1024,1024]{1,0:T(8,128)(2,1)S(1)} fusion(bf16[2048,1024]{1,0:T(8,128)(2,1)S(1)} %copy-done.18, f32[2048,1024]{0,1:T(8,128)} %copy-done.4, f32[1024]{0:T(1024)S(1)} %copy-done.11), kind=kOutput, calls=%fused_computation.32 | convolution fusion | flops 4300210176 | bytes 14684160 | tf_op jit(solution)/shard_map/dot_general | solution.py:41
  128.0 1.6 convert_element_type.68
  129.6 2.0 multiply_reduce_fusion.2
  131.6 2.3 %add_convert_fusion = bf16[512,1024]{0,1:T(8,128)(2,1)S(1)} fusion(bf16[512,1024]{0,1:T(8,128)(2,1)S(1)} %copy-done.5, f32[2048,1024]{0,1:T(8,128)} %copy-done.4, s32[]{:T(128)S(6)} %select_n.2, f32[512,1024]{0,1:T(8,128)S(1)} %convert_element_type.68, f32[512]{0:T(512)S(1)} %get-tuple-element.27, f32[512]{0:T(512)S(1)} %get-tuple-element.28, ...), kind=kLoop, calls=%fused_computation.29 | loop fusion | flops 4718592 | bytes 6303748 | tf_op jit(solution)/shard_map/convert_element_type | solution.py:475
  133.9 1.0 copy-done.9
  134.9 2.8 %convolution_convert_fusion.2 = bf16[512,1024]{1,0:T(8,128)(2,1)} fusion(bf16[512,1024]{0,1:T(8,128)(2,1)S(1)} %add_convert_fusion, bf16[2048,512]{1,0:T(8,128)(2,1)} %copy-done.6, s32[]{:T(128)S(6)} %select_n.2), kind=kOutput, calls=%fused_computation.35 | convolution fusion | flops 537395200 | bytes 2621444 | tf_op jit(solution)/shard_map/dot_general | solution.py:41
  137.7 2.7 %fusion.34 = (f32[512]{0:T(512)S(1)}, f32[512]{0:T(512)S(1)}, f32[512,512]{1,0:T(8,128)S(1)}) fusion(f32[2048,512]{1,0:T(8,128)} %get-tuple-element.22, s32[]{:T(128)S(6)} %select_n.2, f32[512]{0:T(512)S(1)} %copy-done.12, bf16[512,1024]{0,1:T(8,128)(2,1)} %copy-done.9, bf16[512,1024]{1,0:T(8,128)(2,1)} %param.13), kind=kOutput, calls=%fused_computation.67 | convolution fusion | flops 537918464 | bytes 4200452 | tf_op jit(solution)/shard_map/dot_general | solution.py:47
  140.4 1.5 multiply_convert_fusion.6.grad
  142.0 39.8 %backward_exchange.1 = (bf16[2048,128]{1,0:T(8,128)(2,1)S(1)}, f32[128,1024]{1,0:T(8,128)S(1)}) custom-call(bf16[512,512]{1,0:T(8,128)(2,1)S(1)} %multiply_convert_fusion.6.grad, bf16[1024,1024]{1,0:T(8,128)(2,1)S(1)} %convolution_convert_fusion.1.term), custom_call_target="tpu_custom_call" | custom-call | flops 8388608000 | bytes 83886080 | tf_op jit(solution)/shard_map/backward_exchange/pallas_call | solution.py:383
  181.7 5.0 %fusion.16.clone.4 = bf16[2048,128]{1,0:T(8,128)(2,1)S(1)} fusion(bf16[2048,128]{1,0:T(8,128)(2,1)S(1)} %get-tuple-element.13, s32[2048]{0:T(1024)S(1)} %copy-done.15, f32[2048,128]{1,0:T(8,128)S(1)} %copy-done.8), kind=kOutput, calls=%fused_computation.27.clone.clone.clone.1 | convolution fusion | flops 1080557568 | bytes 2105344 | tf_op jit(solution)/shard_map/dot_general | solution.py:41
  186.8 1.7 fusion.18.refs_0_
  188.6 0.9 copy-done.2
  189.5 17.2 %scatter_sum.3 = (f32[128,128]{1,0:T(8,128)S(1)}, f32[64,256]{1,0:T(8,128)S(1)}) custom-call(bf16[1024,128]{1,0:T(8,128)(2,1)S(1)} %fusion.18.refs_0_, bf16[512,256]{1,0:T(8,128)(2,1)S(1)} %copy-done.2), custom_call_target="tpu_custom_call" | custom-call | flops 2097152000 | bytes 20971520 | tf_op jit(solution)/shard_map/scatter_sum/pallas_call | solution.py:413
  208.0 0.8 copy.30
  (54 shorter events, 4.1 us)
Async XLA Ops:
  7.2 42.9 %copy-start = (bf16[1024,1024]{1,0:T(8,128)(2,1)S(1)}, bf16[1024,1024]{1,0:T(8,128)(2,1)}, u32[]{:S(2)}) copy-start(bf16[1024,1024]{1,0:T(8,128)(2,1)} %param.15) | copy-start | bytes 6291460
  7.2 5.4 %copy-start.15 = (s32[2048]{0:T(1024)S(1)}, s32[2048]{0:T(1024)}, u32[]{:S(2)}) copy-start(s32[2048]{0:T(1024)} %param.18) | copy-start | bytes 24580
  7.2 120.8 %reduce-scatter.3.cloned.1.call-start = ((), (), s32[]{:S(2)}) async-start(), calls=%async_computation.2 | async-start | bytes 5242880 | tf_op jit(solution)/shard_map/reduce_scatter | solution.py:464
  11.6 1.0 copy-start.7
  15.7 26.5 %copy-start.12 = (f32[512]{0:T(512)S(1)}, f32[512]{0:T(512)}, u32[]{:S(2)}) copy-start(f32[512]{0:T(512)} %param.12) | copy-start | bytes 6148
  42.2 2.6 %copy-start.14 = (bf16[512,1024]{1,0:T(8,128)(2,1)S(1)}, bf16[512,1024]{1,0:T(8,128)(2,1)}, u32[]{:S(2)}) copy-start(bf16[512,1024]{1,0:T(8,128)(2,1)} %param.13) | copy-start | bytes 3145732
  44.8 2.5 %copy-start.6 = (bf16[2048,512]{1,0:T(8,128)(2,1)}, bf16[2048,512]{1,0:T(8,128)(2,1)S(1)}, u32[]{:S(2)}) copy-start(bf16[2048,512]{1,0:T(8,128)(2,1)S(1)} %get-tuple-element.23) | copy-start | bytes 6291460
  48.2 1.9 copy-start.11
  50.1 5.0 %copy-start.4 = (f32[2048,1024]{0,1:T(8,128)}, f32[2048,1024]{0,1:T(8,128)S(1)}, u32[]{:S(2)}) copy-start(f32[2048,1024]{0,1:T(8,128)S(1)} %subtract_multiply_fusion) | copy-start | bytes 25165828
  50.1 5.2 %copy-start.10 = (bf16[2048,1024]{1,0:T(8,128)(2,1)S(1)}, bf16[2048,1024]{1,0:T(8,128)(2,1)}, u32[]{:S(2)}) copy-start(bf16[2048,1024]{1,0:T(8,128)(2,1)} %param.17) | copy-start | bytes 12582916
  50.1 5.9 %copy-start.13 = (bf16[1024,1024]{1,0:T(8,128)(2,1)S(1)}, bf16[1024,1024]{1,0:T(8,128)(2,1)}, u32[]{:S(2)}) copy-start(bf16[1024,1024]{1,0:T(8,128)(2,1)} %param.16) | copy-start | bytes 6291460
  56.0 8.1 %copy-start.16 = (f32[2048,1024]{1,0:T(8,128)}, f32[2048,1024]{1,0:T(8,128)S(1)}, u32[]{:S(2)}) copy-start(f32[2048,1024]{1,0:T(8,128)S(1)} %fusion.33) | copy-start | bytes 25165828
  64.1 2.0 copy-start.17
  72.2 116.3 %reduce-scatter.5.cloned.1.call-start = ((), (), s32[]{:S(2)}) async-start(), calls=%async_computation.3 | async-start | bytes 1310720 | tf_op jit(solution)/shard_map/reduce_scatter | solution.py:486
  84.3 35.5 %copy-start.18 = (bf16[2048,1024]{1,0:T(8,128)(2,1)S(1)}, bf16[2048,1024]{1,0:T(8,128)(2,1)}, u32[]{:S(2)}) copy-start(bf16[2048,1024]{1,0:T(8,128)(2,1)} %copy-done.17) | copy-start | bytes 12582916
  128.0 3.6 %copy-start.5 = (bf16[512,1024]{0,1:T(8,128)(2,1)S(1)}, bf16[512,1024]{0,1:T(8,128)(2,1)}, u32[]{:S(2)}) copy-start(bf16[512,1024]{0,1:T(8,128)(2,1)} %copy.23) | copy-start | bytes 3145732
  133.9 1.0 copy-start.9
  141.9 39.8 %copy-start.8 = (f32[2048,128]{1,0:T(8,128)S(1)}, f32[2048,128]{1,0:T(8,128)}, u32[]{:S(2)}) copy-start(f32[2048,128]{1,0:T(8,128)} %copy-done.7) | copy-start | bytes 3145732
  181.7 5.0 %copy-start.3 = (bf16[2048,1024]{1,0:T(8,128)(2,1)S(1)}, bf16[2048,1024]{1,0:T(8,128)(2,1)}, u32[]{:S(2)}) copy-start(bf16[2048,1024]{1,0:T(8,128)(2,1)} %param.10) | copy-start | bytes 12582916
  186.8 22.8 %copy-start.1 = (bf16[1024,1024]{1,0:T(8,128)(2,1)S(1)}, bf16[1024,1024]{1,0:T(8,128)(2,1)}, u32[]{:S(2)}) copy-start(bf16[1024,1024]{1,0:T(8,128)(2,1)} %param.15) | copy-start | bytes 6291460
  188.6 1.0 copy-start.2
Sparse Core Ops, SparseCore 0:
  72.4 45.8 reduce-scatter.2
  137.8 24.7 reduce-scatter.4

commit v3 on v2

--- a/solution.py
+++ b/solution.py
@@ -160,6 +160,153 @@
     return pl.ds(pl.multiple_of(index * size, size), size)
 
 
+def product_sum_kernel(parts, count, *refs):
+    pairs = [(refs[2 * i], refs[2 * i + 1]) for i in range(count)]
+    outs = refs[2 * count : 3 * count]
+    made, first_in, staged, second_in = (
+        refs[(3 + i) * count : (4 + i) * count] for i in range(4)
+    )
+    send_one, recv_one, send_two, recv_two = refs[7 * count :]
+    half = parts // 2
+    d = lax.axis_index("dp")
+    parity = lax.rem(d, 2)
+    place = d // 2
+    partner = d + 1 - 2 * parity
+    order = list(range(1, half)) + [0]
+    greet(
+        [("dp", partner)]
+        + [("dp", 2 * lax.rem(place + k, half) + parity) for k in range(1, half)]
+    )
+
+    def make(i, index):
+        left, right = pairs[i]
+        rows = outs[i].shape[0]
+        span = block_of(index, rows)
+        if rows % 128 == 0:
+            piece = left[:, block_of(index, rows)]
+            made[i][span, :] = contract_rows(piece, right[...]).astype(jnp.bfloat16)
+
+    def make_all(i):
+        left, right = pairs[i]
+
+        def step(t, carry):
+            made[i][block_of(t, 128), :] = contract_rows(
+                left[:, block_of(t, 128)], right[...]
+            ).astype(jnp.bfloat16)
+            return carry
+
+        lax.fori_loop(0, left.shape[1] // 128, step, 0)
+
+    def first(i, k):
+        rows = outs[i].shape[0]
+        target = lax.rem(place + k, half)
+        return pltpu.make_async_remote_copy(
+            src_ref=made[i].at[block_of(2 * target + 1 - parity, rows)],
+            dst_ref=first_in[i].at[k],
+            send_sem=send_one.at[i, k],
+            recv_sem=recv_one.at[i, k],
+            device_id={"dp": partner},
+            device_id_type=pl.DeviceIdType.MESH,
+        )
+
+    for i in range(count):
+        whole = outs[i].shape[0] % 128 != 0
+        if whole:
+            make_all(i)
+
+        def send(t, carry, i=i, whole=whole):
+            k = lax.rem(t + 1, half)
+            if not whole:
+                make(i, 2 * lax.rem(place + k, half) + 1 - parity)
+            first(i, k).start()
+            return carry
+
+        lax.fori_loop(0, half, send, 0)
+
+        def keep(t, carry, i=i):
+            make(i, 2 * t + parity)
+            return carry
+
+        if not whole:
+            lax.fori_loop(0, half, keep, 0)
+
+    def each_tile(rows, body):
+        def step(t, carry):
+            body(block_of(t, 16), t)
+            return carry
+
+        lax.fori_loop(0, rows // 16, step, 0)
+
+    twos = {}
+    for i in range(count):
+        for k in order:
+            rows = outs[i].shape[0]
+            target = lax.rem(place + k, half)
+            base = (2 * target + parity) * rows
+            first(i, k).wait_recv()
+
+            def add(tile, step, i=i, k=k, base=base):
+                mine = made[i][pl.ds(pl.multiple_of(base + step * 16, 16), 16), :]
+                total = mine.astype(jnp.float32) + first_in[i][k, tile, :].astype(jnp.float32)
+                if k:
+                    staged[i][k, tile, :] = total.astype(jnp.bfloat16)
+                else:
+                    outs[i][tile, :] = total
+
+            each_tile(rows, add)
+            if k:
+                twos[i, k] = start_copy(
+                    staged[i].at[k],
+                    second_in[i].at[k],
+                    send_two.at[i, k],
+                    recv_two.at[i, k],
+                    "dp",
+                    2 * target + parity,
+                )
+    for i in range(count):
+        for k in range(1, half):
+            twos[i, k].wait_recv()
+
+        def gather(tile, step, i=i):
+            total = outs[i][tile, :]
+            for k in range(1, half):
+                total = total + second_in[i][k, tile, :].astype(jnp.float32)
+            outs[i][tile, :] = total
+
+        each_tile(outs[i].shape[0], gather)
+    for i in range(count):
+        for k in range(half):
+            first(i, k).wait_send()
+    for copy in twos.values():
+        copy.wait_send()
+
+
+def product_sum(pairs, collective_id):
+    parts = lax.axis_size("dp")
+    half = parts // 2
+    count = len(pairs)
+    shapes = [(left.shape[1], right.shape[1]) for left, right in pairs]
+    blocks = [(rows // parts, cols) for rows, cols in shapes]
+    slots = [pltpu.VMEM((half,) + block, jnp.bfloat16) for block in blocks]
+    sent = sum(rows * cols * 2 for rows, cols in shapes)
+    return pl.pallas_call(
+        functools.partial(product_sum_kernel, parts, count),
+        out_shape=[jax.ShapeDtypeStruct(block, jnp.float32) for block in blocks],
+        in_specs=[pl.BlockSpec(memory_space=pltpu.VMEM)] * (2 * count),
+        out_specs=[pl.BlockSpec(memory_space=pltpu.VMEM)] * count,
+        scratch_shapes=[pltpu.VMEM(shape, jnp.bfloat16) for shape in shapes]
+        + slots * 3
+        + [pltpu.SemaphoreType.DMA((count, half))] * 4,
+        compiler_params=pltpu.CompilerParams(
+            collective_id=collective_id, has_side_effects=True, vmem_limit_bytes=VMEM_LIMIT
+        ),
+        cost_estimate=pl.CostEstimate(
+            flops=sent * 4000, bytes_accessed=sent * 40, transcendentals=0
+        ),
+        name="product_sum",
+    )(*[value for pair in pairs for value in pair])
+
+
 def forward_kernel(
     parts, shards, source, packed, arrived, dp_send, dp_recv, near_send, near_recv,
     far_send, far_recv, on_send, on_recv, local
@@ -253,19 +400,12 @@
 
 
 def backward_kernel(
-    parts, shards, grad, term, back, total_out, middle, first_in, staged, second_in,
-    mp_send, mp_recv, dp_send, dp_recv, send_one, recv_one, send_two, recv_two, local
+    parts, shards, grad, back, middle, mp_send, mp_recv, dp_send, dp_recv, local
 ):
     share = grad.shape[0]
     rows, width = back.shape[0] // parts, back.shape[1]
-    out_rows = total_out.shape[0]
-    half = parts // 2
     d = lax.axis_index("dp")
     m = lax.axis_index("mp")
-    parity = lax.rem(d, 2)
-    place = d // 2
-    partner = d + 1 - 2 * parity
-    order = list(range(1, half)) + [0]
     greet(
         [("dp", lax.rem(d + o, parts)) for o in range(1, parts)]
         + [("mp", lax.rem(m + o, shards)) for o in range(1, shards)]
@@ -288,18 +428,6 @@
     )
     own_column.start()
 
-    def pair(k):
-        target = lax.rem(place + k, half)
-        return start_copy(
-            term.at[block_of(2 * target + 1 - parity, out_rows)],
-            first_in.at[k],
-            send_one.at[k],
-            recv_one.at[k],
-            "dp",
-            partner,
-        )
-
-    ones = {order[0]: pair(order[0])}
     for copy in columns:
         copy.wait_recv()
     own_column.wait()
@@ -320,87 +448,31 @@
         middle.at[block_of(d, rows)], back.at[block_of(d, rows)], local.at[1]
     )
     own_block.start()
-    for k in order[1:]:
-        ones[k] = pair(k)
-
-    def each_tile(body):
-        def step(i, carry):
-            body(block_of(i, 16), i)
-            return carry
-
-        lax.fori_loop(0, out_rows // 16, step, 0)
-
-    twos = []
-    for k in order:
-        target = lax.rem(place + k, half)
-        base = (2 * target + parity) * out_rows
-        ones[k].wait_recv()
-
-        def add(tile, step, k=k, base=base):
-            mine = term[pl.ds(pl.multiple_of(base + step * 16, 16), 16), :]
-            total = mine.astype(jnp.float32) + first_in[k, tile, :].astype(jnp.float32)
-            if k:
-                staged[k, tile, :] = total.astype(jnp.bfloat16)
-            else:
-                total_out[tile, :] = total
-
-        each_tile(add)
-        if k:
-            twos.append(
-                start_copy(
-                    staged.at[k],
-                    second_in.at[k],
-                    send_two.at[k],
-                    recv_two.at[k],
-                    "dp",
-                    2 * target + parity,
-                )
-            )
-    for copy in twos:
-        copy.wait_recv()
-
-    def gather(tile, step):
-        total = total_out[tile, :]
-        for k in range(1, half):
-            total = total + second_in[k, tile, :].astype(jnp.float32)
-        total_out[tile, :] = total
-
-    each_tile(gather)
     for copy in blocks:
         copy.wait_recv()
     own_block.wait()
-    for copy in columns + blocks + list(ones.values()) + twos:
+    for copy in columns + blocks:
         copy.wait_send()
 
 
-def backward_exchange(grad, term, collective_id):
+def backward_exchange(grad, collective_id):
     parts, shards = lax.axis_size("dp"), lax.axis_size("mp")
-    half = parts // 2
     share, channels = grad.shape
     back = (share * shards, channels // shards)
-    block = (term.shape[0] // parts, term.shape[1])
-    slots = pltpu.VMEM((half,) + block, jnp.bfloat16)
     return pl.pallas_call(
         functools.partial(backward_kernel, parts, shards),
-        out_shape=[
-            jax.ShapeDtypeStruct(back, grad.dtype),
-            jax.ShapeDtypeStruct(block, jnp.float32),
-        ],
-        in_specs=[pl.BlockSpec(memory_space=pltpu.VMEM)] * 2,
-        out_specs=[pl.BlockSpec(memory_space=pltpu.VMEM)] * 2,
-        scratch_shapes=[pltpu.VMEM(back, grad.dtype), slots, slots, slots]
+        out_shape=jax.ShapeDtypeStruct(back, grad.dtype),
+        in_specs=[pl.BlockSpec(memory_space=pltpu.VMEM)],
+        out_specs=pl.BlockSpec(memory_space=pltpu.VMEM),
+        scratch_shapes=[pltpu.VMEM(back, grad.dtype)]
         + [pltpu.SemaphoreType.DMA((shards,))] * 2
         + [pltpu.SemaphoreType.DMA((parts,))] * 2
-        + [pltpu.SemaphoreType.DMA((half,))] * 4
         + [pltpu.SemaphoreType.DMA((2,))],
         compiler_params=pltpu.CompilerParams(
             collective_id=collective_id, has_side_effects=True, vmem_limit_bytes=VMEM_LIMIT
         ),
-        cost_estimate=pl.CostEstimate(
-            flops=term.size * 8000, bytes_accessed=term.size * 80, transcendentals=0
-        ),
         name="backward_exchange",
-    )(grad, term)
+    )(grad)
 
 
 def scatter_sum(terms, collective_id):
@@ -456,17 +528,14 @@
     active = (valid * gelu_exact(upward)).astype(jnp.bfloat16)
     grad_active = valid * jnp.dot(cotangent, w_out, preferred_element_type=jnp.float32)
     grad_upward = (grad_active * gelu_slope(upward)).astype(jnp.bfloat16)
-    out_term = contract_rows(cotangent, active)
-    in_term = contract_rows(hid_ln, grad_upward)
     partial_value = contract_cols(grad_upward, w_in)
     share_rows = frames // shards
     first_row = member * share_rows
     share_normed = lax.psum_scatter(
         partial_value.astype(jnp.bfloat16), "mp", scatter_dimension=0, tiled=True
     ).astype(jnp.float32)
-    in_term = in_term.astype(jnp.bfloat16)
-    (out_grad,) = scatter_sum([out_term.astype(jnp.bfloat16)], 1)
-    share_normed, in_term, out_grad = lax.optimization_barrier((share_normed, in_term, out_grad))
+    out_grad, in_grad = product_sum([(cotangent, active), (hid_ln, grad_upward)], 1)
+    share_normed, in_grad, out_grad = lax.optimization_barrier((share_normed, in_grad, out_grad))
     share_cot = lax.dynamic_slice_in_dim(valid, first_row, share_rows, 0) * (
         lax.dynamic_slice_in_dim(cotangent, first_row, share_rows, 0).astype(jnp.float32)
     )
@@ -486,7 +555,7 @@
     proj_part = lax.psum_scatter(
         proj_term.astype(jnp.bfloat16), "mp", scatter_dimension=1, tiled=True
     )
-    returned, in_grad = backward_exchange(grad_packed, in_term, 4)
+    returned = backward_exchange(grad_packed, 4)
     grad_features = contract_rows(choose, returned)
     grad_pre = (grad_features * gelu_slope(pre_act)).astype(jnp.bfloat16)
     conv_term = contract_rows(conv_in, grad_pre)

time: 217 us -> 230 us (1.060)
  matrix products: 57.7 us -> 45.9 us
  Pallas kernels: 117 us -> 128 us
  local copies, waits for them, and re-layouts: 11.6 us -> 21.1 us
  other arithmetic: 14.9 us -> 20.4 us
    pallas_call x0 -> x1, Pallas kernels: none -> 63.6 us  [product_sum(): pl.pallas_call(functools.partial(product_sum_kernel, parts, count), out_s...]
    pallas_call x2 -> x1, Pallas kernels: 52.7 us -> 16.5 us  [scatter_sum(): pl.pallas_call(functools.partial(scatter_sum_kernel, parts, count), out_s...]
    dot_general x5 -> x3, matrix products: 26.6 us -> 9.57 us  [contract_rows(): lax.dot_general(left, right, (((0,), (0,)), ((), ())), preferred_element_...]
    pallas_call x1, Pallas kernels: 39.8 us -> 22.8 us  [backward_exchange(): pl.pallas_call(functools.partial(backward_kernel, parts, shards), out_sha...]
    dot_general x0 -> x1, local copies, waits for them, and re-layouts: none -> 9.25 us  [on_device(): hidden = jnp.dot(feat_ln, proj_weight, preferred_element_type=jnp.float32)]
    convert_element_type x0 -> x1, other arithmetic: none -> 3.87 us  [on_device(): hid_ln = (hid_norm * block_gain).astype(jnp.bfloat16)]
    reduce_sum x2, other arithmetic: 1.91 us -> 5.21 us  [normalize(): jnp.mean(centred * centred, axis=-1, keepdims=True) + EPSILON]
    dot_general x1, matrix products: 2.5 us -> 5.61 us  [on_device(): hidden = jnp.dot(feat_ln, proj_weight, preferred_element_type=jnp.float32)]
  transfers between devices with their start and end apart: 2 -> 2, of which waited for: 0 -> 0; matrix products, arithmetic and copies ran while one was open for 14% -> 5% of each run, Pallas kernels for 35% -> 38%
where the time goes in v3:
time: 230 us
  Pallas kernels  128 us (56%)
  matrix products  45.9 us (20%)
  local copies, waits for them, and re-layouts  21.1 us (9%)
  other arithmetic  20.4 us (9%)
  between operations  14.3 us (6%)
    pallas_call x1, Pallas kernels, product_sum(): pl.pallas_call(functools.partial(product_sum_kernel, parts, count), out_s...  63.6 us
    pallas_call x1, Pallas kernels, forward_exchange(): pl.pallas_call(functools.partial(forward_kernel, parts, shards), out_shap...  25 us
    pallas_call x1, Pallas kernels, backward_exchange(): pl.pallas_call(functools.partial(backward_kernel, parts, shards), out_sha...  22.8 us
    pallas_call x1, Pallas kernels, scatter_sum(): pl.pallas_call(functools.partial(scatter_sum_kernel, parts, count), out_s...  16.5 us
    unnamed x40, local copies, waits for them, and re-layouts  11.6 us
    dot_general x3, matrix products, contract_rows(): lax.dot_general(left, right, (((0,), (0,)), ((), ())), preferred_element_...  9.57 us
    dot_general x1, local copies, waits for them, and re-layouts, on_device(): hidden = jnp.dot(feat_ln, proj_weight, preferred_element_type=jnp.float32)  9.25 us
    dot_general x2, matrix products, contract_cols(): lax.dot_general(left, right, (((1,), (1,)), ((), ())), preferred_element_...  9.09 us
  transfers between devices with their start and end apart: 2, of which 0 were waited for; matrix products, arithmetic and copies ran while one was open for 5% of the time, Pallas kernels for 38%

profile of v3, /device:TPU:0, one launch (start us, length us, event | category | flops | bytes accessed | tf_op | source)
XLA Modules:
  0.0 229.8 jit_solution(16263307311313077839)
XLA Ops:
  7.2 0.8 convert_element_type.54
  8.1 3.5 %fusion.31 = f32[2048,128]{1,0:T(8,128)S(1)} fusion(bf16[2048,1024]{1,0:T(8,128)(2,1)} %param.10, bf16[1024,128]{1,0:T(8,128)(2,1)} %param.11), kind=kOutput, calls=%fused_computation.61 | convolution fusion | flops 536870912 | bytes 5505024 | tf_op jit(solution)/shard_map/dot_general | solution.py:516
  11.6 1.0 copy-done.9
  12.6 3.1 %fusion.14.source = bf16[2048,128]{1,0:T(8,128)(2,1)S(1)} fusion(s32[2048]{0:T(1024)S(1)} %copy-done.16, f32[2048,128]{1,0:T(8,128)S(1)} %fusion.31), kind=kOutput, calls=%fused_computation.25 | convolution fusion | flops 1079508992 | bytes 1581056 | tf_op jit(solution)/shard_map/dot_general | solution.py:519
  15.7 25.0 %forward_exchange.1 = bf16[2048,512]{1,0:T(8,128)(2,1)S(1)} custom-call(bf16[2048,128]{1,0:T(8,128)(2,1)S(1)} %fusion.14.source), custom_call_target="tpu_custom_call" | custom-call | tf_op jit(solution)/shard_map/forward_exchange/pallas_call | solution.py:386
  41.1 1.0 fusion.11
  42.2 2.6 %fusion.9 = (f32[2048,512]{1,0:T(8,128)}, bf16[2048,512]{1,0:T(8,128)(2,1)S(1)}) fusion(bf16[2048,512]{1,0:T(8,128)(2,1)S(1)} %forward_exchange.1, f32[2048]{0:T(1024)S(1)} %add_rsqrt_fusion.1, f32[2048]{0:T(1024)S(1)} %broadcast_multiply_fusion.1, f32[512]{0:T(512)S(1)} %copy-done.13), kind=kLoop, calls=%fused_computation.18 | loop fusion | flops 5242880 | bytes 8407040 | tf_op jit(solution)/shard_map/mul | solution.py:30
  44.8 5.6 %fusion.30 = (f32[2048]{0:T(1024)S(1)}, f32[2048,1024]{0,1:T(8,128)}) fusion(bf16[2048,512]{1,0:T(8,128)(2,1)S(1)} %get-tuple-element.25, bf16[512,1024]{1,0:T(8,128)(2,1)S(1)} %copy-done.15), kind=kOutput, calls=%fused_computation.60 | convolution fusion | flops 2149578752 | bytes 11542528 | tf_op jit(solution)/shard_map/dot_general | solution.py:523
  50.4 9.2 %copy.14 = f32[2048,1024]{1,0:T(8,128)} copy(f32[2048,1024]{0,1:T(8,128)} %get-tuple-element.27) | data formatting | bytes 16777216 | tf_op jit(solution)/shard_map/dot_general | solution.py:523
  59.6 4.2 %multiply_reduce_fusion = f32[2048]{0:T(1024)S(1)} fusion(f32[2048,1024]{1,0:T(8,128)} %copy.14, f32[2048]{0:T(1024)S(1)} %broadcast_multiply_fusion), kind=kLoop, calls=%fused_computation.12 | loop fusion | flops 6289408 | bytes 8404992 | tf_op jit(solution)/shard_map/reduce_sum | solution.py:29
  63.9 1.6 copy-done.5
  65.5 3.9 %multiply_convert_fusion.1 = (bf16[2048,1024]{1,0:T(8,128)(2,1)S(1)}, f32[2048,1024]{1,0:T(8,128)}) fusion(f32[1024]{0:T(1024)S(1)} %copy-done.12, f32[2048]{0:T(1024)S(1)} %add_rsqrt_fusion, f32[2048,1024]{1,0:T(8,128)S(1)} %copy-done.5, f32[2048]{0:T(1024)S(1)} %broadcast_multiply_fusion), kind=kLoop, calls=%fused_computation.11 | loop fusion | flops 8388608 | bytes 20992000 | tf_op jit(solution)/shard_map/convert_element_type | solution.py:525
  69.4 7.0 %multiply_convert_fusion = (bf16[2048,1024]{1,0:T(8,128)(2,1)}, f32[2048,1024]{1,0:T(8,128)S(1)}) fusion(f32[2048]{0:T(1024)S(1)} %convert_element_type.54, bf16[2048,1024]{1,0:T(8,128)(2,1)S(1)} %get-tuple-element.22.refs_2_, bf16[1024,1024]{1,0:T(8,128)(2,1)S(1)} %copy-done), kind=kOutput, calls=%fused_computation.9 | convolution fusion | flops 4307550208 | bytes 18882560 | tf_op jit(solution)/shard_map/dot_general | solution.py:526
  76.3 8.1 %fusion.6.refs_3_ = bf16[2048,1024]{1,0:T(8,128)(2,1)S(1)} fusion(f32[2048,1024]{1,0:T(8,128)S(1)} %get-tuple-element.29, bf16[2048,1024]{1,0:T(8,128)(2,1)S(1)} %copy-done.2, bf16[1024,1024]{1,0:T(8,128)(2,1)S(1)} %copy-done.14, f32[2048]{0:T(1024)S(1)} %convert_element_type.54), kind=kOutput, calls=%fused_computation.8 | convolution fusion | flops 4318035968 | bytes 18882560 | tf_op jit(solution)/shard_map/dot_general | solution.py:529
  84.4 1.9 copy-done.17
  86.4 6.3 %convolution_convert_fusion = bf16[2048,1024]{1,0:T(8,128)(2,1)} fusion(bf16[2048,1024]{1,0:T(8,128)(2,1)S(1)} %fusion.6.refs_3_, bf16[1024,1024]{1,0:T(8,128)(2,1)S(1)} %copy-done), kind=kOutput, calls=%fused_computation.22 | convolution fusion | flops 4297064448 | bytes 10485760 | tf_op jit(solution)/shard_map/dot_general | solution.py:47
  92.9 2.2 copy-done.3
  95.1 63.6 %product_sum.1 = (f32[128,1024]{1,0:T(8,128)S(1)}, f32[128,1024]{1,0:T(8,128)S(1)}) custom-call(bf16[2048,1024]{1,0:T(8,128)(2,1)S(1)} %copy-done.3, bf16[2048,1024]{1,0:T(8,128)(2,1)} %get-tuple-element.28.refs_1_, bf16[2048,1024]{1,0:T(8,128)(2,1)} %copy-done.7, bf16[2048,1024]{1,0:T(8,128)(2,1)} %copy-done.17), custom_call_target="tpu_custom_call" | custom-call | flops 16777216000 | bytes 167772160 | tf_op jit(solution)/shard_map/product_sum/pallas_call | solution.py:292
  158.8 1.5 convert_element_type.60
  160.2 2.0 multiply_reduce_fusion.2
  162.3 2.5 %add_convert_fusion = bf16[512,1024]{1,0:T(8,128)(2,1)S(1)} fusion(f32[2048,1024]{1,0:T(8,128)} %get-tuple-element.23, s32[]{:T(128)S(6)} %select_n.2, f32[512,1024]{1,0:T(8,128)S(1)} %convert_element_type.60, f32[512]{0:T(512)S(1)} %get-tuple-element.31, f32[512]{0:T(512)S(1)} %get-tuple-element.32, f32[1024]{0:T(1024)S(1)} %copy-done.12, ...), kind=kLoop, calls=%fused_computation.26 | loop fusion | flops 4718592 | bytes 6303748 | tf_op jit(solution)/shard_map/convert_element_type | solution.py:544
  164.8 1.0 copy-done.11
  165.8 2.8 %convolution_convert_fusion.1 = bf16[512,1024]{1,0:T(8,128)(2,1)} fusion(bf16[512,1024]{1,0:T(8,128)(2,1)S(1)} %add_convert_fusion, bf16[2048,512]{1,0:T(8,128)(2,1)} %copy-done.8, s32[]{:T(128)S(6)} %select_n.2), kind=kOutput, calls=%fused_computation.30 | convolution fusion | flops 537395200 | bytes 2621444 | tf_op jit(solution)/shard_map/dot_general | solution.py:41
  168.6 2.8 %fusion.29 = (f32[512]{0:T(512)S(1)}, f32[512]{0:T(512)S(1)}, f32[512,512]{1,0:T(8,128)S(1)}) fusion(f32[2048,512]{1,0:T(8,128)} %get-tuple-element.24, s32[]{:T(128)S(6)} %select_n.2, f32[512]{0:T(512)S(1)} %copy-done.13, bf16[512,1024]{1,0:T(8,128)(2,1)} %copy-done.11, bf16[512,1024]{1,0:T(8,128)(2,1)} %param.13), kind=kOutput, calls=%fused_computation.59 | convolution fusion | flops 537918464 | bytes 4200452 | tf_op jit(solution)/shard_map/dot_general | solution.py:47
  171.5 1.5 multiply_convert_fusion.3.grad
  173.0 22.8 %backward_exchange.1 = bf16[2048,128]{1,0:T(8,128)(2,1)S(1)} custom-call(bf16[512,512]{1,0:T(8,128)(2,1)S(1)} %multiply_convert_fusion.3.grad), custom_call_target="tpu_custom_call" | custom-call | tf_op jit(solution)/shard_map/backward_exchange/pallas_call | solution.py:462
  195.8 5.0 %fusion.13.clone.4 = bf16[2048,128]{1,0:T(8,128)(2,1)S(1)} fusion(bf16[2048,128]{1,0:T(8,128)(2,1)S(1)} %backward_exchange.1, s32[2048]{0:T(1024)S(1)} %copy-done.16, f32[2048,128]{1,0:T(8,128)S(1)} %copy-done.10), kind=kOutput, calls=%fused_computation.24.clone.clone.clone.1 | convolution fusion | flops 1080557568 | bytes 2105344 | tf_op jit(solution)/shard_map/dot_general | solution.py:41
  200.8 1.8 fusion.15.refs_0_
  202.7 0.9 copy-done.4
  203.6 16.5 %scatter_sum.1 = (f32[128,128]{1,0:T(8,128)S(1)}, f32[64,256]{1,0:T(8,128)S(1)}) custom-call(bf16[1024,128]{1,0:T(8,128)(2,1)S(1)} %fusion.15.refs_0_, bf16[512,256]{1,0:T(8,128)(2,1)S(1)} %copy-done.4), custom_call_target="tpu_custom_call" | custom-call | flops 2097152000 | bytes 20971520 | tf_op jit(solution)/shard_map/scatter_sum/pallas_call | solution.py:485
  221.3 0.8 copy.25
  222.1 0.8 copy.26
  (49 shorter events, 2.1 us)
Async XLA Ops:
  7.2 62.2 %copy-start = (bf16[1024,1024]{1,0:T(8,128)(2,1)S(1)}, bf16[1024,1024]{1,0:T(8,128)(2,1)}, u32[]{:S(2)}) copy-start(bf16[1024,1024]{1,0:T(8,128)(2,1)} %param.15) | copy-start | bytes 6291460
  7.2 5.4 %copy-start.16 = (s32[2048]{0:T(1024)S(1)}, s32[2048]{0:T(1024)}, u32[]{:S(2)}) copy-start(s32[2048]{0:T(1024)} %param.18) | copy-start | bytes 24580
  7.2 151.6 %reduce-scatter.3.cloned.1.call-start = ((), (), s32[]{:S(2)}) async-start(), calls=%async_computation.2 | async-start | bytes 5242880 | tf_op jit(solution)/shard_map/reduce_scatter | solution.py:534
  11.6 1.0 copy-start.9
  15.7 26.5 %copy-start.13 = (f32[512]{0:T(512)S(1)}, f32[512]{0:T(512)}, u32[]{:S(2)}) copy-start(f32[512]{0:T(512)} %param.12) | copy-start | bytes 6148
  42.2 2.6 %copy-start.15 = (bf16[512,1024]{1,0:T(8,128)(2,1)S(1)}, bf16[512,1024]{1,0:T(8,128)(2,1)}, u32[]{:S(2)}) copy-start(bf16[512,1024]{1,0:T(8,128)(2,1)} %param.13) | copy-start | bytes 3145732
  44.8 5.6 %copy-start.8 = (bf16[2048,512]{1,0:T(8,128)(2,1)}, bf16[2048,512]{1,0:T(8,128)(2,1)S(1)}, u32[]{:S(2)}) copy-start(bf16[2048,512]{1,0:T(8,128)(2,1)S(1)} %get-tuple-element.25) | copy-start | bytes 6291460
  59.6 5.8 %copy-start.5 = (f32[2048,1024]{1,0:T(8,128)S(1)}, f32[2048,1024]{1,0:T(8,128)}, u32[]{:S(2)}) copy-start(f32[2048,1024]{1,0:T(8,128)} %copy.14) | copy-start | bytes 25165828
  59.6 5.8 %copy-start.12 = (f32[1024]{0:T(1024)S(1)}, f32[1024]{0:T(1024)}, u32[]{:S(2)}) copy-start(f32[1024]{0:T(1024)} %param.14) | copy-start | bytes 12292
  69.4 7.0 %copy-start.7 = (bf16[2048,1024]{1,0:T(8,128)(2,1)}, bf16[2048,1024]{1,0:T(8,128)(2,1)S(1)}, u32[]{:S(2)}) copy-start(bf16[2048,1024]{1,0:T(8,128)(2,1)S(1)} %get-tuple-element.22.refs_2_) | copy-start | bytes 12582916
  69.4 7.0 %copy-start.2 = (bf16[2048,1024]{1,0:T(8,128)(2,1)S(1)}, bf16[2048,1024]{1,0:T(8,128)(2,1)}, u32[]{:S(2)}) copy-start(bf16[2048,1024]{1,0:T(8,128)(2,1)} %refs_0_.1) | copy-start | bytes 12582916
  69.4 7.0 %copy-start.14 = (bf16[1024,1024]{1,0:T(8,128)(2,1)S(1)}, bf16[1024,1024]{1,0:T(8,128)(2,1)}, u32[]{:S(2)}) copy-start(bf16[1024,1024]{1,0:T(8,128)(2,1)} %param.16) | copy-start | bytes 6291460
  84.4 1.9 copy-start.17
  92.7 109.9 %reduce-scatter.5.cloned.1.call-start = ((), (), s32[]{:S(2)}) async-start(), calls=%async_computation.3 | async-start | bytes 1310720 | tf_op jit(solution)/shard_map/reduce_scatter | solution.py:555
  92.9 2.2 copy-start.3
  164.8 1.0 copy-start.11
  168.6 27.2 %copy-start.10 = (f32[2048,128]{1,0:T(8,128)S(1)}, f32[2048,128]{1,0:T(8,128)}, u32[]{:S(2)}) copy-start(f32[2048,128]{1,0:T(8,128)} %copy-done.9) | copy-start | bytes 3145732
  195.8 5.0 %copy-start.6 = (bf16[2048,1024]{1,0:T(8,128)(2,1)S(1)}, bf16[2048,1024]{1,0:T(8,128)(2,1)}, u32[]{:S(2)}) copy-start(bf16[2048,1024]{1,0:T(8,128)(2,1)} %param.10) | copy-start | bytes 12582916
  200.8 22.1 %copy-start.1 = (bf16[1024,1024]{1,0:T(8,128)(2,1)S(1)}, bf16[1024,1024]{1,0:T(8,128)(2,1)}, u32[]{:S(2)}) copy-start(bf16[1024,1024]{1,0:T(8,128)(2,1)} %param.15) | copy-start | bytes 6291460
  202.6 1.0 copy-start.4
Sparse Core Ops, SparseCore 0:
  92.8 46.0 reduce-scatter.2
  168.7 29.3 reduce-scatter.4

commit v4 on v3

--- a/solution.py
+++ b/solution.py
@@ -132,6 +132,49 @@
         each_tile(outs[i].shape[0], gather)
     for copy in list(ones.values()) + list(twos.values()):
         copy.wait_send()
+
+
+def norms_kernel(
+    packed, gain_feat, weight, gain_block, feat_norm, feat_inv, feat_ln, hid_norm, hid_inv, hid_ln
+):
+    normed, inv = normalize(packed[...].astype(jnp.float32))
+    feat_norm[...] = normed
+    feat_inv[...] = inv
+    scaled = (normed * gain_feat[...]).astype(jnp.bfloat16)
+    feat_ln[...] = scaled
+    hidden = jnp.dot(scaled, weight[...], preferred_element_type=jnp.float32)
+    normed, inv = normalize(hidden)
+    hid_norm[...] = normed
+    hid_inv[...] = inv
+    hid_ln[...] = (normed * gain_block[...]).astype(jnp.bfloat16)
+
+
+def norms(packed, gain_feat, weight, gain_block):
+    rows, channels = packed.shape
+    width = weight.shape[1]
+    step = min(256, rows)
+
+    def by_row(size):
+        return pl.BlockSpec((step, size), lambda i: (i, 0))
+
+    def whole(*shape):
+        return pl.BlockSpec(shape, lambda i: (0, 0))
+
+    def made(size, kind):
+        return jax.ShapeDtypeStruct((rows, size), kind)
+
+    return pl.pallas_call(
+        norms_kernel,
+        grid=(rows // step,),
+        out_shape=[
+            made(channels, jnp.float32), made(1, jnp.float32), made(channels, jnp.bfloat16),
+            made(width, jnp.float32), made(1, jnp.float32), made(width, jnp.bfloat16),
+        ],
+        in_specs=[by_row(channels), whole(1, channels), whole(channels, width), whole(1, width)],
+        out_specs=[by_row(size) for size in (channels, 1, channels, width, 1, width)],
+        compiler_params=pltpu.CompilerParams(vmem_limit_bytes=VMEM_LIMIT // 2),
+        name="norms",
+    )(packed, gain_feat[None, :], weight, gain_block[None, :])
 
 
 def start_copy(src, dst, send_sem, recv_sem, axis, index):
@@ -518,11 +561,9 @@
     choose = (send_index[:, None] == jnp.arange(frames, dtype=send_index.dtype)).astype(jnp.bfloat16)
     outgoing = jnp.dot(choose, features, preferred_element_type=jnp.float32).astype(jnp.bfloat16)
     packed = forward_exchange(outgoing, 3)
-    feat_norm, feat_inv = normalize(packed.astype(jnp.float32))
-    feat_ln = (feat_norm * feature_gain).astype(jnp.bfloat16)
-    hidden = jnp.dot(feat_ln, proj_weight, preferred_element_type=jnp.float32)
-    hid_norm, hid_inv = normalize(hidden)
-    hid_ln = (hid_norm * block_gain).astype(jnp.bfloat16)
+    feat_norm, feat_inv, feat_ln, hid_norm, hid_inv, hid_ln = norms(
+        packed, feature_gain, proj_weight, block_gain
+    )
     upward = jnp.dot(hid_ln, w_in, preferred_element_type=jnp.float32)
     valid = slot_valid.astype(jnp.float32)[:, None]
     active = (valid * gelu_exact(upward)).astype(jnp.bfloat16)

time: 230 us -> 216 us (0.939)
  other arithmetic: 20.4 us -> 8.72 us
  Pallas kernels: 128 us -> 136 us
  matrix products: 45.9 us -> 39.6 us
  local copies, waits for them, and re-layouts: 21.1 us -> 16.6 us
    dot_general x1 -> x0, local copies, waits for them, and re-layouts: 9.25 us -> none  [on_device(): hidden = jnp.dot(feat_ln, proj_weight, preferred_element_type=jnp.float32)]
    pallas_call x0 -> x1, Pallas kernels: none -> 7.47 us  [norms(): pl.pallas_call(norms_kernel, grid=(rows // step,), out_shape=[made(channe...]
    dot_general x1 -> x0, matrix products: 5.61 us -> none  [on_device(): hidden = jnp.dot(feat_ln, proj_weight, preferred_element_type=jnp.float32)]
    reduce_sum x3 -> x0, other arithmetic: 5.56 us -> none  [the longest x2 5.21 us: normalize(): jnp.mean(centred * centred, axis=-1, keepdims=True) + EPSILON]
    convert_element_type x1 -> x0, other arithmetic: 3.87 us -> none  [on_device(): hid_ln = (hid_norm * block_gain).astype(jnp.bfloat16)]
    unnamed x40 -> x52, local copies, waits for them, and re-layouts: 11.6 us -> 14.3 us
    mul x1 -> x0, other arithmetic: 2.56 us -> none  [normalize(): return (centred * inv_std, inv_std)]
  transfers between devices with their start and end apart: 2 -> 2, of which waited for: 0 -> 0; matrix products, arithmetic and copies ran while one was open for 5% -> 6% of each run, Pallas kernels for 38% -> 40%
where the time goes in v4:
time: 216 us; the launch traced here: 215 us
  Pallas kernels  136 us (63%)
  matrix products  39.6 us (18%)
  local copies, waits for them, and re-layouts  16.6 us (8%)
  between operations  14.4 us (7%)
  other arithmetic  8.72 us (4%)
    pallas_call x1, Pallas kernels, product_sum(): pl.pallas_call(functools.partial(product_sum_kernel, parts, count), out_s...  64.1 us
    pallas_call x1, Pallas kernels, forward_exchange(): pl.pallas_call(functools.partial(forward_kernel, parts, shards), out_shap...  25 us
    pallas_call x1, Pallas kernels, backward_exchange(): pl.pallas_call(functools.partial(backward_kernel, parts, shards), out_sha...  22.8 us
    pallas_call x1, Pallas kernels, scatter_sum(): pl.pallas_call(functools.partial(scatter_sum_kernel, parts, count), out_s...  16.3 us
    unnamed x52, local copies, waits for them, and re-layouts  14.3 us
    dot_general x3, matrix products, contract_rows(): lax.dot_general(left, right, (((0,), (0,)), ((), ())), preferred_element_...  9.55 us
    dot_general x2, matrix products, contract_cols(): lax.dot_general(left, right, (((1,), (1,)), ((), ())), preferred_element_...  8.41 us
    dot_general x1, matrix products, on_device(): jnp.dot(cotangent, w_out, preferred_element_type=jnp.float32)  8.03 us
  transfers between devices with their start and end apart: 2, of which 0 were waited for; matrix products, arithmetic and copies ran while one was open for 6% of the time, Pallas kernels for 40%

profile of v4, /device:TPU:0, one launch (start us, length us, event | category | flops | bytes accessed | tf_op | source)
XLA Modules:
  0.0 215.4 jit_solution(11522430567217706543)
XLA Ops:
  7.2 0.8 convert_element_type.44
  8.1 3.5 %fusion.27 = f32[2048,128]{1,0:T(8,128)S(1)} fusion(bf16[2048,1024]{1,0:T(8,128)(2,1)} %param.10, bf16[1024,128]{1,0:T(8,128)(2,1)} %param.11), kind=kOutput, calls=%fused_computation.49 | convolution fusion | flops 536870912 | bytes 5505024 | tf_op jit(solution)/shard_map/dot_general | solution.py:559
  11.6 3.1 %fusion.11.source = bf16[2048,128]{1,0:T(8,128)(2,1)S(1)} fusion(s32[2048]{0:T(1024)S(1)} %copy-done.22, f32[2048,128]{1,0:T(8,128)S(1)} %fusion.27), kind=kOutput, calls=%fused_computation.16 | convolution fusion | flops 1079508992 | bytes 1581056 | tf_op jit(solution)/shard_map/dot_general | solution.py:562
  14.8 25.0 %forward_exchange.1.packed = bf16[2048,512]{1,0:T(8,128)(2,1)S(1)} custom-call(bf16[2048,128]{1,0:T(8,128)(2,1)S(1)} %fusion.11.source), custom_call_target="tpu_custom_call" | custom-call | tf_op jit(solution)/shard_map/forward_exchange/pallas_call | solution.py:429
  39.8 7.5 %norms.1 = (f32[2048,512]{1,0:T(8,128)S(1)}, f32[2048,1]{1,0:T(8,128)S(1)}, bf16[2048,512]{1,0:T(8,128)(2,1)S(1)}, f32[2048,1024]{1,0:T(8,128)S(1)}, f32[2048,1]...) custom-call(bf16[2048,512]{1,0:T(8,128)(2,1)S(1)} %forward_exchange.1.packed, f32[1,512]{1,0:T(1,128)S(1)} %bitcast.24, ...), custom_call_target="tpu_custom_call" | custom-call | tf_op jit(solution)/shard_map/norms/pallas_call | solution.py:166
  47.3 3.2 %copy-done.2 = f32[2048,1024]{1,0:T(8,128)} copy-done((f32[2048,1024]{1,0:T(8,128)}, f32[2048,1024]{1,0:T(8,128)S(1)}, u32[]{:S(2)}) %copy-start.2) | copy-done | bytes 8388632
  50.6 2.0 copy-done.8
  52.5 1.0 copy-done.11
  53.5 7.0 %multiply_convert_fusion = (bf16[2048,1024]{1,0:T(8,128)(2,1)}, f32[2048,1024]{1,0:T(8,128)S(1)}) fusion(f32[2048]{0:T(1024)S(1)} %convert_element_type.44, bf16[2048,1024]{1,0:T(8,128)(2,1)S(1)} %get-tuple-element.19.refs_2_, bf16[1024,1024]{1,0:T(8,128)(2,1)S(1)} %copy-done), kind=kOutput, calls=%fused_computation.9 | convolution fusion | flops 4307550208 | bytes 18882560 | tf_op jit(solution)/shard_map/dot_general | solution.py:567
  60.6 8.0 %fusion.6.refs_3_ = bf16[2048,1024]{1,0:T(8,128)(2,1)S(1)} fusion(f32[2048,1024]{1,0:T(8,128)S(1)} %get-tuple-element.35, bf16[2048,1024]{1,0:T(8,128)(2,1)S(1)} %copy-done.9, bf16[1024,1024]{1,0:T(8,128)(2,1)S(1)} %copy-done.21, f32[2048]{0:T(1024)S(1)} %convert_element_type.44), kind=kOutput, calls=%fused_computation.8 | convolution fusion | flops 4318035968 | bytes 18882560 | tf_op jit(solution)/shard_map/dot_general | solution.py:570
  68.6 2.0 copy-done.23
  70.6 6.3 %convolution_convert_fusion = bf16[2048,1024]{1,0:T(8,128)(2,1)} fusion(bf16[2048,1024]{1,0:T(8,128)(2,1)S(1)} %fusion.6.refs_3_, bf16[1024,1024]{1,0:T(8,128)(2,1)S(1)} %copy-done), kind=kOutput, calls=%fused_computation.13 | convolution fusion | flops 4297064448 | bytes 10485760 | tf_op jit(solution)/shard_map/dot_general | solution.py:47
  76.9 0.2 reduce-scatter.5.cloned.1.call-start
  77.2 1.1 dynamic-slice_reduce_fusion
  78.3 2.2 %copy-done.10 = bf16[2048,1024]{1,0:T(8,128)(2,1)S(1)} copy-done((bf16[2048,1024]{1,0:T(8,128)(2,1)S(1)}, bf16[2048,1024]{1,0:T(8,128)(2,1)}, u32[]{:S(2)}) %copy-start.10) | copy-done | bytes 4194328
  80.5 64.1 %product_sum.1 = (f32[128,1024]{1,0:T(8,128)S(1)}, f32[128,1024]{1,0:T(8,128)S(1)}) custom-call(bf16[2048,1024]{1,0:T(8,128)(2,1)S(1)} %copy-done.10, bf16[2048,1024]{1,0:T(8,128)(2,1)} %get-tuple-element.34.refs_1_, bf16[2048,1024]{1,0:T(8,128)(2,1)} %copy-done.15, bf16[2048,1024]{1,0:T(8,128)(2,1)} %copy-done.23), custom_call_target="tpu_custom_call" | custom-call | flops 16777216000 | bytes 167772160 | tf_op jit(solution)/shard_map/product_sum/pallas_call | solution.py:335
  144.7 1.8 convert_element_type.48
  146.5 2.0 multiply_reduce_fusion.1
  148.5 2.5 %add_convert_fusion = bf16[512,1024]{1,0:T(8,128)(2,1)S(1)} fusion(f32[2048,1024]{1,0:T(8,128)} %copy-done.2, s32[]{:T(128)S(6)} %select_n.2, f32[512,1024]{1,0:T(8,128)S(1)} %convert_element_type.48, f32[512]{0:T(512)S(1)} %get-tuple-element.37, f32[512]{0:T(512)S(1)} %get-tuple-element.38, f32[1024]{0:T(1024)S(1)} %copy-done.13, ...), kind=kLoop, calls=%fused_computation.17 | loop fusion | flops 4718592 | bytes 6303748 | tf_op jit(solution)/shard_map/convert_element_type | solution.py:585
  151.1 2.8 %convolution_convert_fusion.1 = bf16[512,1024]{1,0:T(8,128)(2,1)} fusion(bf16[512,1024]{1,0:T(8,128)(2,1)S(1)} %add_convert_fusion, bf16[2048,512]{1,0:T(8,128)(2,1)} %copy-done.16, s32[]{:T(128)S(6)} %select_n.2), kind=kOutput, calls=%fused_computation.21 | convolution fusion | flops 537395200 | bytes 2621444 | tf_op jit(solution)/shard_map/dot_general | solution.py:41
  153.9 1.2 dynamic-slice_reduce_fusion.1
  155.0 2.1 fusion.26
  157.2 1.5 multiply_convert_fusion.1.grad
  158.7 22.8 %backward_exchange.1 = bf16[2048,128]{1,0:T(8,128)(2,1)S(1)} custom-call(bf16[512,512]{1,0:T(8,128)(2,1)S(1)} %multiply_convert_fusion.1.grad), custom_call_target="tpu_custom_call" | custom-call | tf_op jit(solution)/shard_map/backward_exchange/pallas_call | solution.py:505
  181.5 5.0 %fusion.10.clone.4 = bf16[2048,128]{1,0:T(8,128)(2,1)S(1)} fusion(bf16[2048,128]{1,0:T(8,128)(2,1)S(1)} %backward_exchange.1, s32[2048]{0:T(1024)S(1)} %copy-done.22, f32[2048,128]{1,0:T(8,128)S(1)} %copy-done.20), kind=kOutput, calls=%fused_computation.15.clone.clone.clone.1 | convolution fusion | flops 1080557568 | bytes 2105344 | tf_op jit(solution)/shard_map/dot_general | solution.py:41
  186.6 1.8 fusion.12.refs_0_
  188.4 1.0 copy-done.17
  189.4 16.3 %scatter_sum.1 = (f32[128,128]{1,0:T(8,128)S(1)}, f32[64,256]{1,0:T(8,128)S(1)}) custom-call(bf16[1024,128]{1,0:T(8,128)(2,1)S(1)} %fusion.12.refs_0_, bf16[512,256]{1,0:T(8,128)(2,1)S(1)} %copy-done.17), custom_call_target="tpu_custom_call" | custom-call | flops 2097152000 | bytes 20971520 | tf_op jit(solution)/shard_map/scatter_sum/pallas_call | solution.py:528
  205.7 0.6 copy.24
  206.3 0.6 copy.25
  207.0 0.8 copy.26
  207.7 0.8 copy.27
  (51 shorter events, 0.3 us)
Async XLA Ops:
  7.2 46.3 %copy-start = (bf16[1024,1024]{1,0:T(8,128)(2,1)S(1)}, bf16[1024,1024]{1,0:T(8,128)(2,1)}, u32[]{:S(2)}) copy-start(bf16[1024,1024]{1,0:T(8,128)(2,1)} %param.15) | copy-start | bytes 6291460
  7.2 4.4 %copy-start.22 = (s32[2048]{0:T(1024)S(1)}, s32[2048]{0:T(1024)}, u32[]{:S(2)}) copy-start(s32[2048]{0:T(1024)} %param.18) | copy-start | bytes 24580
  7.2 137.5 %reduce-scatter.3.cloned.1.call-start = ((), (), s32[]{:S(2)}) async-start(), calls=%async_computation.2 | async-start | bytes 5242880 | tf_op jit(solution)/shard_map/reduce_scatter | solution.py:575
  11.6 3.2 %copy-start.19 = (f32[2048,128]{1,0:T(8,128)}, f32[2048,128]{1,0:T(8,128)S(1)}, u32[]{:S(2)}) copy-start(f32[2048,128]{1,0:T(8,128)S(1)} %fusion.27) | copy-start | bytes 3145732
  11.6 28.3 %copy-start.3 = (bf16[512,1024]{1,0:T(8,128)(2,1)S(1)}, bf16[512,1024]{1,0:T(8,128)(2,1)}, u32[]{:S(2)}) copy-start(bf16[512,1024]{1,0:T(8,128)(2,1)} %weight.1) | copy-start | bytes 3145732
  11.6 28.3 %copy-start.13 = (f32[1024]{0:T(1024)S(1)}, f32[1024]{0:T(1024)}, u32[]{:S(2)}) copy-start(f32[1024]{0:T(1024)} %param.14) | copy-start | bytes 12292
  11.6 28.3 %copy-start.14 = (f32[512]{0:T(512)S(1)}, f32[512]{0:T(512)}, u32[]{:S(2)}) copy-start(f32[512]{0:T(512)} %param.12) | copy-start | bytes 6148
  47.3 3.2 %copy-start.2 = (f32[2048,1024]{1,0:T(8,128)}, f32[2048,1024]{1,0:T(8,128)S(1)}, u32[]{:S(2)}) copy-start(f32[2048,1024]{1,0:T(8,128)S(1)} %get-tuple-element.23) | copy-start | bytes 25165828
  50.6 2.0 copy-start.8
  52.5 1.0 copy-start.11
  53.5 7.0 %copy-start.12 = (f32[2048,1]{1,0:T(8,128)}, f32[2048,1]{1,0:T(8,128)S(1)}, u32[]{:S(2)}) copy-start(f32[2048,1]{1,0:T(8,128)S(1)} %get-tuple-element.18) | copy-start | bytes 24580
  53.5 7.0 %copy-start.15 = (bf16[2048,1024]{1,0:T(8,128)(2,1)}, bf16[2048,1024]{1,0:T(8,128)(2,1)S(1)}, u32[]{:S(2)}) copy-start(bf16[2048,1024]{1,0:T(8,128)(2,1)S(1)} %get-tuple-element.19.refs_2_) | copy-start | bytes 12582916
  53.5 7.0 %copy-start.16 = (bf16[2048,512]{1,0:T(8,128)(2,1)}, bf16[2048,512]{1,0:T(8,128)(2,1)S(1)}, u32[]{:S(2)}) copy-start(bf16[2048,512]{1,0:T(8,128)(2,1)S(1)} %get-tuple-element.25) | copy-start | bytes 6291460
  53.5 7.0 %copy-start.9 = (bf16[2048,1024]{1,0:T(8,128)(2,1)S(1)}, bf16[2048,1024]{1,0:T(8,128)(2,1)}, u32[]{:S(2)}) copy-start(bf16[2048,1024]{1,0:T(8,128)(2,1)} %refs_0_.1) | copy-start | bytes 12582916
  53.5 7.0 %copy-start.21 = (bf16[1024,1024]{1,0:T(8,128)(2,1)S(1)}, bf16[1024,1024]{1,0:T(8,128)(2,1)}, u32[]{:S(2)}) copy-start(bf16[1024,1024]{1,0:T(8,128)(2,1)} %param.16) | copy-start | bytes 6291460
  68.6 2.0 copy-start.23
  76.9 111.5 %reduce-scatter.5.cloned.1.call-start = ((), (), s32[]{:S(2)}) async-start(), calls=%async_computation.3 | async-start | bytes 1310720 | tf_op jit(solution)/shard_map/reduce_scatter | solution.py:596
  78.3 2.2 %copy-start.10 = (bf16[2048,1024]{1,0:T(8,128)(2,1)S(1)}, bf16[2048,1024]{1,0:T(8,128)(2,1)}, u32[]{:S(2)}) copy-start(bf16[2048,1024]{1,0:T(8,128)(2,1)} %refs_0_.1) | copy-start | bytes 12582916
  144.6 6.4 %copy-start.4 = (f32[128,1024]{1,0:T(8,128)}, f32[128,1024]{1,0:T(8,128)S(1)}, u32[]{:S(2)}) copy-start(f32[128,1024]{1,0:T(8,128)S(1)} %get-tuple-element.46) | copy-start | bytes 1572868
  144.6 6.4 %copy-start.6 = (f32[128,1024]{1,0:T(8,128)}, f32[128,1024]{1,0:T(8,128)S(1)}, u32[]{:S(2)}) copy-start(f32[128,1024]{1,0:T(8,128)S(1)} %get-tuple-element.45) | copy-start | bytes 1572868
  153.8 27.6 %copy-start.20 = (f32[2048,128]{1,0:T(8,128)S(1)}, f32[2048,128]{1,0:T(8,128)}, u32[]{:S(2)}) copy-start(f32[2048,128]{1,0:T(8,128)} %copy-done.19) | copy-start | bytes 3145732
  181.5 5.0 %copy-start.18 = (bf16[2048,1024]{1,0:T(8,128)(2,1)S(1)}, bf16[2048,1024]{1,0:T(8,128)(2,1)}, u32[]{:S(2)}) copy-start(bf16[2048,1024]{1,0:T(8,128)(2,1)} %param.10) | copy-start | bytes 12582916
  186.5 22.0 %copy-start.1 = (bf16[1024,1024]{1,0:T(8,128)(2,1)S(1)}, bf16[1024,1024]{1,0:T(8,128)(2,1)}, u32[]{:S(2)}) copy-start(bf16[1024,1024]{1,0:T(8,128)(2,1)} %param.15) | copy-start | bytes 6291460
  188.3 18.6 %copy-start.7 = (f32[128,1024]{1,0:T(8,128)S(1)}, f32[128,1024]{1,0:T(8,128)}, u32[]{:S(2)}) copy-start(f32[128,1024]{1,0:T(8,128)} %copy-done.6) | copy-start | bytes 1572868
  188.3 19.4 %copy-start.5 = (f32[128,1024]{1,0:T(8,128)S(1)}, f32[128,1024]{1,0:T(8,128)}, u32[]{:S(2)}) copy-start(f32[128,1024]{1,0:T(8,128)} %copy-done.4) | copy-start | bytes 1572868
  188.4 1.0 copy-start.17
Sparse Core Ops, SparseCore 0:
  77.0 46.0 reduce-scatter.2
  154.0 29.1 reduce-scatter.4
